TPU v7x, 32 devices: a whole 2x2x4 slice. The times are simulated.
32 devices in a mesh: group: 4 (over y, core), dom: 8 (over z, x).
Axes of the slice: x: 2, y: 2, z: 4, core: 2. Of those that a mesh axis runs over, the one named last changes fastest.
Arguments:
- hidden: bfloat16 [32768, 512], P(('group', 'dom')), may hold values from -6 to 6
- enc_weight: bfloat16 [512, 512], replicated, may hold values from -0.25 to 0.25
- enc_bias: float32 [512], replicated, may hold values from -3 to 3
- enc_slope: float32 [512], replicated, may hold values from 0.05 to 0.5
- dec_token: bfloat16 [512], replicated, may hold values from -4 to 4
- dec_weight: bfloat16 [512, 128], replicated, may hold values from -0.25 to 0.25
- dec_bias: float32 [128], replicated, may hold values from -3 to 3
- targets: bfloat16 [32768, 128], P(('group', 'dom')), may hold values from -6 to 6
- local_tiles: bfloat16 [384, 128, 128], P(('group', 'dom')), may hold values from -0.375 to 0.375
- local_src: int32 [32, 12], P(('group', 'dom')), may hold values from 0 to 7
- local_dst: int32 [32, 12], P(('group', 'dom')), may hold values from 0 to 7
- local_count: int32 [32], P(('group', 'dom')), may hold values from 4 to 12, as said below
- halo_tiles: bfloat16 [256, 128, 128], P(('group', 'dom')), may hold values from -0.375 to 0.375
- halo_src: int32 [32, 8], P(('group', 'dom')), may hold values from 0 to 7, each once within a row
- halo_dst: int32 [32, 8], P(('group', 'dom')), may hold values from 0 to 7
- send_rows: int32 [256, 64], P(('group', 'dom')), may hold values from 0 to 1023
- cross_rows: int32 [128, 128], P(('group', 'dom')), may hold values from 0 to 1023
- mask_nodes: int32 [32, 512], P(('group', 'dom')), may hold values from 0 to 1023, as said below
- remask_nodes: int32 [32, 256], P(('group', 'dom')), may hold values from 0 to 1023, as said below
Outputs:
- rebuilt: bfloat16 [32768, 128], P(('group', 'dom'))
- node_error: float32 [32768], P(('group', 'dom'))
Inputs may be any that keep to these rules, and one draw needn't show every extreme that they name: `local_count`: live local tiles of a partition; tile slots at or past it are ignored; some partition has 12. `halo_src`: each partition's row names each of its boundary blocks once. `mask_nodes`: distinct rows within a partition. `remask_nodes`: distinct rows within a partition.
All inputs are finite; a program needn't handle non-finite values.
Results may differ from a plain program's by a relative error of at most 0.0056.
Values may be sent and summed in bfloat16 or wider, within the bound.
No kernel may reach another device: no remote copies, remote signals or barrier semaphores. Data moves between devices by JAX's collectives and lax.ppermute only.
A program may use at most 64 MiB of HBM per device.

v0:
```python
import functools

import jax
import jax.numpy as jnp
from jax import lax
from jax.experimental import pallas as pl
from jax.experimental.pallas import tpu as pltpu
from jax.sharding import PartitionSpec as P


F32 = jnp.float32
BF16 = jnp.bfloat16
VMEM = pl.BlockSpec(memory_space=pltpu.VMEM)
HBM = pl.BlockSpec(memory_space=pltpu.HBM)
SMEM = pl.BlockSpec(memory_space=pltpu.SMEM)
GRANT = 24 << 20


class Axis:
    def __init__(self, name, size):
        self.name, self.size = name, size
        self.inner = 2 if size % 2 == 0 else 1
        self.outer = size // self.inner

    def turn(self, place, step, size, back=False):
        if size & (size - 1) == 0:
            return place ^ step
        return (place + (size - step if back else step)) % size

    def partner(self, me, step, back=False):
        outer = self.turn(me // self.inner, step // self.inner, self.outer, back)
        inner = self.turn(me % self.inner, step % self.inner, self.inner, back)
        return outer * self.inner + inner

    def permute(self, x, step):
        return lax.ppermute(x, self.name, [(j, self.partner(j, step)) for j in range(self.size)])


def mm(a, b):
    return jnp.dot(a, b, preferred_element_type=F32)


def column(row):
    m = row.shape[1]
    here = lax.broadcasted_iota(jnp.int32, (m, m), 0)
    there = lax.broadcasted_iota(jnp.int32, (m, m), 1)
    return jnp.sum(jnp.where(here == there, row.astype(F32), 0.0), axis=1, keepdims=True)


def as_row(col):
    m = col.shape[0]
    here = lax.broadcasted_iota(jnp.int32, (m, m), 0)
    there = lax.broadcasted_iota(jnp.int32, (m, m), 1)
    return jnp.sum(jnp.where(here == there, col, 0.0), axis=0, keepdims=True)


def one_hot(ids, width):
    spots = lax.broadcasted_iota(jnp.int32, (ids.shape[0], width), 1)
    return jnp.where(spots == ids, 1.0, 0.0).astype(BF16)


def listed(nodes, start, rows):
    spots = lax.broadcasted_iota(jnp.int32, (rows, nodes.shape[1]), 0) + start
    return jnp.max(jnp.where(spots == nodes, 1.0, 0.0), axis=1, keepdims=True)


def span(block, size):
    return pl.ds(pl.multiple_of(block * size, size), size)


def start_copies(pairs, sems, first=0):
    made = [pltpu.make_async_copy(a, b, sems.at[first + i]) for i, (a, b) in enumerate(pairs)]
    for copy in made:
        copy.start()
    return made


def wait_copies(made):
    for copy in made:
        copy.wait()


def slot_ids(axis, listing, steps):
    me = lax.axis_index(axis.name)
    for step in steps:
        ids = listing[pl.ds(axis.partner(me, step), 1), :]
        yield column(ids).astype(jnp.int32)


def encode_kernel(axes, n_staged, chunks, *refs):
    dom, grp = axes
    hidden_h, weight_h, send_h, cross_h = refs[:4]
    staged_h = refs[4 : 4 + n_staged]
    outs = refs[4 + n_staged : -4]
    hidden, weight, picks, sems = refs[-4:]
    encoded, send_rows, cross_rows = outs[:3]
    n = dom.size + grp.size - 2
    sends, staged = outs[3 : 3 + n], outs[3 + n :]
    rows = hidden.shape[0]
    spans = [pl.ds(i * (rows // chunks), rows // chunks) for i in range(chunks)]
    pairs = [(send_h, send_rows), (cross_h, cross_rows), (weight_h, weight)]
    pairs += [(hidden_h.at[s], hidden.at[s]) for s in spans]
    made = start_copies(pairs, sems)
    later = start_copies(list(zip(staged_h, staged)), sems, len(pairs))
    at = 0
    for axis, listing, copy in ((dom, send_rows, made[0]), (grp, cross_rows, made[1])):
        copy.wait()
        for ids in slot_ids(axis, listing, range(1, axis.size)):
            picks[at : at + ids.shape[0], :] = one_hot(ids, rows)
            at += ids.shape[0]
    made[2].wait()
    for i, s in enumerate(spans):
        made[3 + i].wait()
        encoded[s, :] = mm(hidden[s, :], weight[...]).astype(BF16)
    got = mm(picks[...], encoded[...]).astype(BF16)
    at = 0
    for send in sends:
        m = send.shape[0]
        send[...] = got[at : at + m, :]
        at += m
    wait_copies(later)


def add_tiles(total, parts, source, tiles, src, dst, count=None):
    n, blk = tiles.shape[:2]
    for t in range(n):
        tile = tiles[t]
        if count is not None:
            tile = jnp.where(t < count[0], tile, jnp.zeros_like(tile))
        parts[t] = mm(tile, source[span(src[0, t], blk), :])
    for t in range(n):
        total[span(dst[0, t], blk), :] += parts[t]


def local_kernel(axes, encoded, tiles, src_v, dst_v, bias, remask, send_rows, cross_rows, count, *refs):
    total, folded, upper, masked, *stay = refs[:-4]
    parts, src, dst, sems = refs[-4:]
    made = start_copies([(src_v, src), (dst_v, dst)], sems)
    blk = tiles.shape[1]
    rows = encoded.shape[0]
    half = folded.shape[1]
    total[...] = jnp.broadcast_to(bias[...], total.shape)
    at = 0
    for axis, listing, out in zip(axes, (send_rows, cross_rows), stay):
        for step, ids in enumerate(slot_ids(axis, listing, range(axis.size))):
            m = ids.shape[0]
            over = ids >= half
            folded[at : at + m, :] = one_hot(jnp.where(over, ids - half, ids), half)
            upper[at : at + m, :] = jnp.broadcast_to(jnp.where(over, 1.0, 0.0), (m, upper.shape[1]))
            if step == 0:
                out[...] = mm(one_hot(ids, rows), encoded[...]).astype(BF16)
            at += m
    for n in range(rows // blk):
        hit = listed(remask[...], n * blk, blk)
        masked[n * blk : (n + 1) * blk, :] = jnp.broadcast_to(hit, (blk, masked.shape[1]))
    wait_copies(made)
    add_tiles(total, parts, encoded, tiles, src, dst, count)


def latent_kernel(axes, total, tiles, src_v, dst_v, folded, upper, masked, slope, token, weight, *rest):
    dom, grp = axes
    n = dom.size + grp.size
    got, outs = rest[:n], rest[n:-6]
    summed, pool, parts, src, dst, sems = rest[-6:]
    made = start_copies([(src_v, src), (dst_v, dst)], sems)
    at = 0
    for axis, mine in ((dom, got[: dom.size]), (grp, got[dom.size :])):
        me = lax.axis_index(axis.name)
        m = mine[0].shape[0]
        for step, part in enumerate(mine):
            start = at + axis.partner(me, step, back=True) * m
            pool[pl.ds(pl.multiple_of(start, m), m), :] = part[...]
        at += axis.size * m
    summed[...] = total[...]
    shared = jnp.broadcast_to(token[...].reshape(1, -1).astype(F32), (16, token.shape[0])).astype(BF16)
    replaced = mm(shared, weight[...])[0:1, :]
    wait_copies(made)
    add_tiles(summed, parts, pool, tiles, src, dst)
    narrowed = outs[0]
    latent = jnp.maximum(summed[...], slope[...] * summed[...]).astype(BF16)
    narrowed[...] = jnp.where(masked[...] > 0, replaced, mm(latent, weight[...])).astype(BF16)
    half, narrow = folded.shape[1], narrowed.shape[1]
    both = jnp.concatenate([narrowed[:half, :], narrowed[half:, :]], axis=1)
    pair = mm(folded[...], both)
    sent = jnp.where(upper[...] > 0, pair[:, narrow:], pair[:, :narrow]).astype(BF16)
    at, out = 0, 1
    for axis, mine in ((dom, got[: dom.size]), (grp, got[dom.size :])):
        m = mine[0].shape[0]
        for size in [m] * axis.inner + [axis.inner * m] * (axis.outer - 1):
            outs[out][...] = sent[at : at + size, :]
            at, out = at + size, out + 1


def narrow_local_kernel(narrowed, tiles, src_v, dst_v, bias, count, total, parts, src, dst, sems):
    made = start_copies([(src_v, src), (dst_v, dst)], sems)
    total[...] = jnp.broadcast_to(bias[...], total.shape)
    wait_copies(made)
    add_tiles(total, parts, narrowed, tiles, src, dst, count)


def target_kernel(blk, targets, nodes, scale, wanted):
    for n in range(scale.shape[0]):
        x = targets[n * blk : (n + 1) * blk, :].astype(F32)
        power = as_row(jnp.mean(x * x, axis=1, keepdims=True))
        scale[n : n + 1, :] = lax.rsqrt(power + 1e-06)
        wanted[n : n + 1, :] = as_row(listed(nodes[...], n * blk, blk))


def forward_kernel(axes, *refs):
    at = 0
    outs = refs[sum(axis.outer for axis in axes) :]
    for axis, out in zip(axes, outs):
        m = refs[at].shape[0]
        out[0:m, :] = refs[at][...]
        for outer in range(1, axis.outer):
            out[outer * m : (outer + 1) * m, :] = refs[at + outer][m : 2 * m, :]
        at += axis.outer


def final_kernel(axes, total, tiles, src_v, dst_v, targets, scale, wanted, *rest):
    rebuilt, error, summed, pool, parts, src, dst, sems = rest[-8:]
    made = start_copies([(src_v, src), (dst_v, dst)], sems)
    blk = tiles.shape[1]
    at, ref = 0, 0
    for axis in axes:
        me = lax.axis_index(axis.name)
        stay, outer_got = rest[ref], rest[ref + 1 : ref + axis.outer]
        ref += axis.outer
        m = stay.shape[0]
        pieces = [(0, stay, 0)]
        pieces += [((1 + i) * axis.inner, got, 0) for i, got in enumerate(outer_got)]
        if axis.inner > 1:
            pieces += [(i * axis.inner + 1, rest[ref], i * m) for i in range(axis.outer)]
            ref += 1
        for step, got, where in pieces:
            start = at + axis.partner(me, step, back=True) * m
            pool[pl.ds(pl.multiple_of(start, m), m), :] = got[where : where + m, :]
        at += axis.size * m
    summed[...] = total[...]
    wait_copies(made)
    add_tiles(summed, parts, pool, tiles, src, dst)
    for b in range(scale.shape[0]):
        rounded = summed[b * blk : (b + 1) * blk, :].astype(BF16)
        rebuilt[b * blk : (b + 1) * blk, :] = rounded
        u = rounded.astype(F32)
        x = targets[b * blk : (b + 1) * blk, :].astype(F32)
        dots = as_row(jnp.mean(u * x, axis=1, keepdims=True))
        power = as_row(jnp.mean(u * u, axis=1, keepdims=True))
        cosine = dots * lax.rsqrt(power + 1e-06) * scale[b : b + 1, :]
        error[b : b + 1, :] = jnp.where(wanted[b : b + 1, :] > 0, (1.0 - cosine) ** 2, 0.0)


def call(kernel, outs, specs, args, scratch=(), flops=10**9):
    return pl.pallas_call(
        kernel,
        out_shape=tuple(outs),
        in_specs=specs,
        out_specs=tuple(VMEM for _ in outs),
        scratch_shapes=scratch,
        compiler_params=pltpu.CompilerParams(vmem_limit_bytes=GRANT),
        cost_estimate=pl.CostEstimate(flops=flops, bytes_accessed=2**20, transcendentals=0),
    )(*args)


def per_device(
    n_grp,
    n_dom,
    hidden,
    enc_weight,
    enc_bias,
    enc_slope,
    dec_token,
    dec_weight,
    dec_bias,
    targets,
    local_tiles,
    local_src,
    local_dst,
    local_count,
    halo_tiles,
    halo_src,
    halo_dst,
    send_rows,
    cross_rows,
    mask_nodes,
    remask_nodes,
):
    sds = jax.ShapeDtypeStruct
    i32 = jnp.int32
    rows, width = hidden.shape
    narrow = dec_weight.shape[1]
    n_tiles, blk = local_tiles.shape[:2]
    n_halo = halo_tiles.shape[0]
    blocks = rows // blk
    m_dom, m_grp = send_rows.shape[1], cross_rows.shape[1]
    halo_rows = n_dom * m_dom + n_grp * m_grp
    dom, grp = axes = (Axis("dom", n_dom), Axis("group", n_grp))
    chunks = 4
    to_stage = (
        local_tiles,
        local_src,
        local_dst,
        halo_tiles,
        halo_src,
        halo_dst,
        enc_bias[None, :],
        enc_slope[None, :],
        dec_token,
        dec_weight,
        dec_bias[None, :],
        targets,
        mask_nodes,
        remask_nodes,
    )

    def like(arrays):
        return [sds(x.shape, x.dtype) for x in arrays]

    def scalars(*arrays):
        return [pltpu.SMEM(x.shape, i32) for x in arrays] + [pltpu.SemaphoreType.DMA((len(arrays),))]

    fed = [pltpu.with_memory_space_constraint(x, pltpu.HBM) for x in (hidden, enc_weight, send_rows, cross_rows, *to_stage)]
    slots = [sds((m_dom, width), BF16)] * (n_dom - 1) + [sds((m_grp, width), BF16)] * (n_grp - 1)
    encoded, send_rows, cross_rows, *outs = call(
        functools.partial(encode_kernel, axes, len(to_stage), chunks),
        [sds((rows, width), BF16)] + like((send_rows, cross_rows)) + slots + like(to_stage),
        [HBM] * len(fed),
        fed,
        [
            pltpu.VMEM(hidden.shape, BF16),
            pltpu.VMEM(enc_weight.shape, BF16),
            pltpu.VMEM(((n_dom - 1) * m_dom + (n_grp - 1) * m_grp, rows), BF16),
            pltpu.SemaphoreType.DMA((3 + chunks + len(to_stage),)),
        ],
    )
    sends, staged = outs[: len(slots)], outs[len(slots) :]
    tiles, src, dst, halo_edges, halo_from, halo_to = staged[:6]
    enc_bias, enc_slope, dec_token, dec_weight, dec_bias, targets, mask_nodes, remask_nodes = staged[6:]
    dom_got = [dom.permute(sends[s - 1], s) for s in range(1, n_dom)]
    grp_got = [grp.permute(sends[n_dom + s - 2], s) for s in range(1, n_grp)]

    total, folded, upper, masked, dom_stay, grp_stay = call(
        functools.partial(local_kernel, axes),
        [
            sds((rows, width), F32),
            sds((halo_rows, rows // 2), BF16),
            sds((halo_rows, narrow), F32),
            sds((rows, narrow), F32),
            sds((m_dom, width), BF16),
            sds((m_grp, width), BF16),
        ],
        [VMEM] * 8 + [SMEM],
        (encoded, tiles, src, dst, enc_bias, remask_nodes, send_rows, cross_rows, local_count),
        [pltpu.VMEM((n_tiles, blk, width), F32)] + scalars(src, dst),
    )
    slots = []
    for axis, m in ((dom, m_dom), (grp, m_grp)):
        slots += [sds((m, narrow), BF16)] * axis.inner
        slots += [sds((axis.inner * m, narrow), BF16)] * (axis.outer - 1)
    args = (total, halo_edges, halo_from, halo_to, folded, upper, masked, enc_slope, dec_token, dec_weight)
    args += (dom_stay, *dom_got, grp_stay, *grp_got)
    narrowed, *outs = call(
        functools.partial(latent_kernel, axes),
        [sds((rows, narrow), BF16)] + slots,
        [VMEM] * len(args),
        args,
        [pltpu.VMEM((rows, width), F32), pltpu.VMEM((halo_rows, width), BF16), pltpu.VMEM((n_halo, blk, width), F32)]
        + scalars(halo_from, halo_to),
    )
    stay, passing, outer_got = [], [], []
    for axis in axes:
        stay.append(outs[0])
        passing.append(outs[1 : axis.inner])
        rest, outs = outs[axis.inner : axis.inner + axis.outer - 1], outs[axis.inner + axis.outer - 1 :]
        outer_got.append([axis.permute(x, (i + 1) * axis.inner) for i, x in enumerate(rest)])
    (total,) = call(
        narrow_local_kernel,
        [sds((rows, narrow), F32)],
        [VMEM] * 5 + [SMEM],
        (narrowed, tiles, src, dst, dec_bias, local_count),
        [pltpu.VMEM((n_tiles, blk, narrow), F32)] + scalars(src, dst),
    )
    scale, wanted = call(
        functools.partial(target_kernel, blk),
        [sds((blocks, blk), F32), sds((blocks, blk), F32)],
        [VMEM] * 2,
        (targets, mask_nodes),
    )
    split = [i for i, axis in enumerate(axes) if axis.inner > 1]
    inner_got = [[], []]
    if split:
        args = [x for i in split for x in (*passing[i], *outer_got[i])]
        forward = call(
            functools.partial(forward_kernel, [axes[i] for i in split]),
            [sds((axes[i].outer * (m_dom, m_grp)[i], narrow), BF16) for i in split],
            [VMEM] * len(args),
            args,
            flops=10**7,
        )
        for i, x in zip(split, forward):
            inner_got[i] = [axes[i].permute(x, 1)]
    got = [x for i in range(2) for x in (stay[i], *outer_got[i], *inner_got[i])]
    rebuilt, error = call(
        functools.partial(final_kernel, axes),
        [sds((rows, narrow), BF16), sds((blocks, blk), F32)],
        [VMEM] * (7 + len(got)),
        (total, halo_edges, halo_from, halo_to, targets, scale, wanted, *got),
        [pltpu.VMEM((rows, narrow), F32), pltpu.VMEM((halo_rows, narrow), BF16), pltpu.VMEM((n_halo, blk, narrow), F32)]
        + scalars(halo_from, halo_to),
    )
    return rebuilt, error.reshape(-1)


def solution(mesh):
    split = ("group", "dom")
    in_specs = (
        P(split, None),
        P(),
        P(),
        P(),
        P(),
        P(),
        P(),
        P(split, None),
        P(split, None, None),
        P(split, None),
        P(split, None),
        P(split),
        P(split, None, None),
        P(split, None),
        P(split, None),
        P(split, None),
        P(split, None),
        P(split, None),
        P(split, None),
    )
    out_specs = (P(split, None), P(split))
    sizes = mesh.shape["group"], mesh.shape["dom"]

    def body(*args):
        return per_device(*sizes, *args)

    return jax.shard_map(body, mesh=mesh, in_specs=in_specs, out_specs=out_specs, check_vma=False)
```

profile of v0, /device:TPU:0, one launch (start us, length us, event | category | flops | bytes accessed | tf_op | source)
XLA Modules:
  0.0 45.2 jit_solution(4657651843813238074)
XLA Ops:
  0.6 3.6 %shard_map.194 = (bf16[1024,512]{1,0:T(8,128)(2,1)S(1)}, s32[8,64]{1,0:T(8,128)S(1)}, s32[4,128]{1,0:T(4,128)S(1)}, bf16[64,512]{1,0:T(8,128)(2,1)S(1)}, bf16[64...) custom-call(bf16[1024,512]{1,0:T(8,128)(2,1)} %refs_0_.1, ...), custom_call_target="tpu_custom_call" | custom-call | flops 1000000000 | bytes 1048576 | tf_op jit(solution)/shard_map/pallas_call | solution.py:254
  4.2 3.0 %collective-permute-start = (bf16[64,512]{1,0:T(8,128)(2,1)S(1)}, bf16[64,512]{1,0:T(8,128)(2,1)S(1)}, u32[]{:S(2)}, u32[]{:S(2)}) collective-permute-start(bf16[64,512]{1,0:T(8,128)(2,1)S(1)} %get-tuple-element.69), channel_id=1, source_target_pairs={{0,1},{1,0},{2,3},{3,2},{4,5},{5,4},{6,7},{7,6},{8,9},{9,8},{10,11... | collective-permute-start | bytes 196616 | tf_op jit(solution)/shard_map/ppermute | solution.py:36
  7.3 1.6 %collective-permute-start.1 = (bf16[64,512]{1,0:T(8,128)(2,1)S(1)}, bf16[64,512]{1,0:T(8,128)(2,1)S(1)}, u32[]{:S(2)}, u32[]{:S(2)}) collective-permute-start(bf16[64,512]{1,0:T(8,128)(2,1)S(1)} %get-tuple-element.70), channel_id=1, source_target_pairs={{0,2},{1,3},{2,0},{3,1},{4,6},{5,7},{6,4},{7,5},{8,10},{9,11},{10,... | collective-permute-start | bytes 196616 | tf_op jit(solution)/shard_map/ppermute | solution.py:36
  8.8 0.0 collective-permute-start.2
  8.8 3.0 %collective-permute-start.3 = (bf16[64,512]{1,0:T(8,128)(2,1)S(1)}, bf16[64,512]{1,0:T(8,128)(2,1)S(1)}, u32[]{:S(2)}, u32[]{:S(2)}) collective-permute-start(bf16[64,512]{1,0:T(8,128)(2,1)S(1)} %get-tuple-element.72), channel_id=1, source_target_pairs={{0,4},{1,5},{2,6},{3,7},{4,0},{5,1},{6,2},{7,3},{8,12},{9,13},{10,... | collective-permute-start | bytes 196616 | tf_op jit(solution)/shard_map/ppermute | solution.py:36
  11.9 1.3 %collective-permute-start.4 = (bf16[64,512]{1,0:T(8,128)(2,1)S(1)}, bf16[64,512]{1,0:T(8,128)(2,1)S(1)}, u32[]{:S(2)}, u32[]{:S(2)}) collective-permute-start(bf16[64,512]{1,0:T(8,128)(2,1)S(1)} %get-tuple-element.73), channel_id=1, source_target_pairs={{0,5},{1,4},{2,7},{3,6},{4,1},{5,0},{6,3},{7,2},{8,13},{9,12},{10,... | collective-permute-start | bytes 196616 | tf_op jit(solution)/shard_map/ppermute | solution.py:36
  13.1 0.0 collective-permute-done.rest_1_
  13.1 0.0 collective-permute-start.7
  13.1 0.0 collective-permute-done.1.rest_2_
  13.1 1.6 %collective-permute-start.8 = (bf16[128,512]{1,0:T(8,128)(2,1)S(1)}, bf16[128,512]{1,0:T(8,128)(2,1)S(1)}, u32[]{:S(2)}, u32[]{:S(2)}) collective-permute-start(bf16[128,512]{1,0:T(8,128)(2,1)S(1)} %get-tuple-element.78), channel_id=1, source_target_pairs={{0,16},{8,24},{16,0},{24,8},{1,17},{9,25},{17,1},{25,9},{2,18},{10... | collective-permute-start | bytes 393224 | tf_op jit(solution)/shard_map/ppermute | solution.py:36
  14.7 0.3 collective-permute-start.9
  15.6 0.0 collective-permute-done.3.rest_4_
  15.7 4.4 %collective-permute-start.5 = (bf16[64,512]{1,0:T(8,128)(2,1)S(1)}, bf16[64,512]{1,0:T(8,128)(2,1)S(1)}, u32[]{:S(2)}, u32[]{:S(2)}) collective-permute-start(bf16[64,512]{1,0:T(8,128)(2,1)S(1)} %get-tuple-element.74), channel_id=1, source_target_pairs={{0,6},{1,7},{2,4},{3,5},{4,2},{5,3},{6,0},{7,1},{8,14},{9,15},{10,... | collective-permute-start | bytes 196616 | tf_op jit(solution)/shard_map/ppermute | solution.py:36
  20.0 0.0 collective-permute-done.4.rest_5_
  20.0 1.8 %collective-permute-start.6 = (bf16[64,512]{1,0:T(8,128)(2,1)S(1)}, bf16[64,512]{1,0:T(8,128)(2,1)S(1)}, u32[]{:S(2)}, u32[]{:S(2)}) collective-permute-start(bf16[64,512]{1,0:T(8,128)(2,1)S(1)} %get-tuple-element.75), channel_id=1, source_target_pairs={{0,7},{1,6},{2,5},{3,4},{4,3},{5,2},{6,1},{7,0},{8,15},{9,14},{10,... | collective-permute-start | bytes 196616 | tf_op jit(solution)/shard_map/ppermute | solution.py:36
  21.8 1.5 %shard_map.195 = (f32[1024,512]{1,0:T(8,128)S(1)}, bf16[1024,512]{1,0:T(8,128)(2,1)S(1)}, f32[1024,128]{1,0:T(8,128)S(1)}, f32[1024,128]{1,0:T(8,128)S(1)}, bf16...) custom-call(bf16[1024,512]{1,0:T(8,128)(2,1)S(1)} %get-tuple-element.50.encoded, ...), custom_call_target="tpu_custom_call" | custom-call | flops 1000000000 | bytes 1048576 | tf_op jit(solution)/shard_map/pallas_call | solution.py:254
  23.4 0.0 collective-permute-done.5.rest_6_
  23.4 3.6 %collective-permute-done.6.rest_7_ = bf16[64,512]{1,0:T(8,128)(2,1)S(1)} collective-permute-done((bf16[64,512]{1,0:T(8,128)(2,1)S(1)}, bf16[64,512]{1,0:T(8,128)(2,1)S(1)}, u32[]{:S(2)}, u32[]{:S(2)}) %collective-permute-start.6) | collective-permute-done | bytes 65568 | tf_op jit(solution)/shard_map/ppermute | solution.py:36
  27.0 0.0 collective-permute-done.7.rest_9_
  27.0 0.0 collective-permute-done.8.rest_10_
  27.0 0.0 collective-permute-done.9.rest_11_
  27.0 2.4 %shard_map.196 = (bf16[1024,128]{1,0:T(8,128)(2,1)S(1)}, bf16[64,128]{1,0:T(8,128)(2,1)S(1)}, bf16[64,128]{1,0:T(8,128)(2,1)S(1)}, bf16[128,128]{1,0:T(8,128)(2,...) custom-call(f32[1024,512]{1,0:T(8,128)S(1)} %get-tuple-element.58.to, ...), custom_call_target="tpu_custom_call" | custom-call | flops 1000000000 | bytes 1048576 | tf_op jit(solution)/shard_map/pallas_call | solution.py:254
  29.4 1.6 %collective-permute-start.13 = (bf16[256,128]{1,0:T(8,128)(2,1)S(1)}, bf16[256,128]{1,0:T(8,128)(2,1)S(1)}, u32[]{:S(2)}, u32[]{:S(2)}) collective-permute-start(bf16[256,128]{1,0:T(8,128)(2,1)S(1)} %get-tuple-element.92), channel_id=1, source_target_pairs={{0,16},{8,24},{16,0},{24,8},{1,17},{9,25},{17,1},{25,9},{2,18},{10... | collective-permute-start | bytes 196616 | tf_op jit(solution)/shard_map/ppermute | solution.py:36
  31.0 2.4 %collective-permute-start.11 = (bf16[128,128]{1,0:T(8,128)(2,1)S(1)}, bf16[128,128]{1,0:T(8,128)(2,1)S(1)}, u32[]{:S(2)}, u32[]{:S(2)}) collective-permute-start(bf16[128,128]{1,0:T(8,128)(2,1)S(1)} %get-tuple-element.88), channel_id=1, source_target_pairs={{0,4},{1,5},{2,6},{3,7},{4,0},{5,1},{6,2},{7,3},{8,12},{9,13},{10,... | collective-permute-start | bytes 98312 | tf_op jit(solution)/shard_map/ppermute | solution.py:36
  33.4 2.0 %collective-permute-start.12 = (bf16[128,128]{1,0:T(8,128)(2,1)S(1)}, bf16[128,128]{1,0:T(8,128)(2,1)S(1)}, u32[]{:S(2)}, u32[]{:S(2)}) collective-permute-start(bf16[128,128]{1,0:T(8,128)(2,1)S(1)} %get-tuple-element.89), channel_id=1, source_target_pairs={{0,6},{1,7},{2,4},{3,5},{4,2},{5,3},{6,0},{7,1},{8,14},{9,15},{10,... | collective-permute-start | bytes 98312 | tf_op jit(solution)/shard_map/ppermute | solution.py:36
  35.4 0.4 shard_map.198
  35.8 0.4 collective-permute-done.11.refs_2_.rest_2_
  36.2 2.9 %collective-permute-done.12.refs_3_.rest_3_ = bf16[128,128]{1,0:T(8,128)(2,1)S(1)} collective-permute-done((bf16[128,128]{1,0:T(8,128)(2,1)S(1)}, bf16[128,128]{1,0:T(8,128)(2,1)S(1)}, u32[]{:S(2)}, u32[]{:S(2)}) %collective-permute-start.12) | collective-permute-done | bytes 32800 | tf_op jit(solution)/shard_map/ppermute | solution.py:36
  39.1 0.6 %collective-permute-start.14 = (bf16[256,128]{1,0:T(8,128)(2,1)S(1)}, bf16[256,128]{1,0:T(8,128)(2,1)S(1)}, u32[]{:S(2)}, u32[]{:S(2)}) collective-permute-start(bf16[256,128]{1,0:T(8,128)(2,1)S(1)} %get-tuple-element.93), channel_id=1, source_target_pairs={{0,1},{1,0},{2,3},{3,2},{4,5},{5,4},{6,7},{7,6},{8,9},{9,8},{10,11... | collective-permute-start | bytes 196616 | tf_op jit(solution)/shard_map/ppermute | solution.py:36
  39.7 0.9 %shard_map.197.total = f32[1024,128]{1,0:T(8,128)S(1)} custom-call(bf16[1024,128]{1,0:T(8,128)(2,1)S(1)} %get-tuple-element.80.narrowed, bf16[12,128,128]{2,1,0:T(8,128)(2,1)S(1)} %get-tuple-element.51.tiles, s32[1,12]{1,0:T(1,128)S(1)} %get-tuple-element.52.src_v, s32[1,12]{1,0:T(1,128)S(1)} %get-tuple-element.53.dst_v, ...), custom_call_target="tpu_custom_call" | custom-call | flops 1000000000 | bytes 1048576 | tf_op jit(solution)/shard_map/pallas_call | solution.py:254
  40.6 2.9 %collective-permute-done.14.rest_4_ = bf16[256,128]{1,0:T(8,128)(2,1)S(1)} collective-permute-done((bf16[256,128]{1,0:T(8,128)(2,1)S(1)}, bf16[256,128]{1,0:T(8,128)(2,1)S(1)}, u32[]{:S(2)}, u32[]{:S(2)}) %collective-permute-start.14) | collective-permute-done | bytes 65568 | tf_op jit(solution)/shard_map/ppermute | solution.py:36
  43.4 1.8 %shard_map.200 = (bf16[1024,128]{1,0:T(8,128)(2,1)}, f32[8,128]{1,0:T(8,128)}) custom-call(f32[1024,128]{1,0:T(8,128)S(1)} %shard_map.197.total, bf16[8,128,128]{2,1,0:T(8,128)(2,1)S(1)} %get-tuple-element.59.tiles, s32[1,8]{1,0:T(1,128)S(1)} %get-tuple-element.60.src_v, s32[1,8]{1,0:T(1,128)S(1)} %get-tuple-element.61.dst_v, ...), custom_call_target="tpu_custom_call" | custom-call | flops 1000000000 | bytes 1048576 | tf_op jit(solution)/shard_map/pallas_call | solution.py:254
  (7 shorter events, 0.0 us)
Async XLA Ops:
  4.2 8.9 %collective-permute-start = (bf16[64,512]{1,0:T(8,128)(2,1)S(1)}, bf16[64,512]{1,0:T(8,128)(2,1)S(1)}, u32[]{:S(2)}, u32[]{:S(2)}) collective-permute-start(bf16[64,512]{1,0:T(8,128)(2,1)S(1)} %get-tuple-element.69), channel_id=1, source_target_pairs={{0,1},{1,0},{2,3},{3,2},{4,5},{5,4},{6,7},{7,6},{8,9},{9,8},{10,11... | collective-permute-start | bytes 196616 | tf_op jit(solution)/shard_map/ppermute | solution.py:36
  7.3 5.9 %collective-permute-start.1 = (bf16[64,512]{1,0:T(8,128)(2,1)S(1)}, bf16[64,512]{1,0:T(8,128)(2,1)S(1)}, u32[]{:S(2)}, u32[]{:S(2)}) collective-permute-start(bf16[64,512]{1,0:T(8,128)(2,1)S(1)} %get-tuple-element.70), channel_id=1, source_target_pairs={{0,2},{1,3},{2,0},{3,1},{4,6},{5,7},{6,4},{7,5},{8,10},{9,11},{10,... | collective-permute-start | bytes 196616 | tf_op jit(solution)/shard_map/ppermute | solution.py:36
  8.8 5.9 %collective-permute-start.2 = (bf16[64,512]{1,0:T(8,128)(2,1)S(1)}, bf16[64,512]{1,0:T(8,128)(2,1)S(1)}, u32[]{:S(2)}, u32[]{:S(2)}) collective-permute-start(bf16[64,512]{1,0:T(8,128)(2,1)S(1)} %get-tuple-element.71), channel_id=1, source_target_pairs={{0,3},{1,2},{2,1},{3,0},{4,7},{5,6},{6,5},{7,4},{8,11},{9,10},{10,... | collective-permute-start | bytes 196616 | tf_op jit(solution)/shard_map/ppermute | solution.py:36
  8.8 6.8 %collective-permute-start.3 = (bf16[64,512]{1,0:T(8,128)(2,1)S(1)}, bf16[64,512]{1,0:T(8,128)(2,1)S(1)}, u32[]{:S(2)}, u32[]{:S(2)}) collective-permute-start(bf16[64,512]{1,0:T(8,128)(2,1)S(1)} %get-tuple-element.72), channel_id=1, source_target_pairs={{0,4},{1,5},{2,6},{3,7},{4,0},{5,1},{6,2},{7,3},{8,12},{9,13},{10,... | collective-permute-start | bytes 196616 | tf_op jit(solution)/shard_map/ppermute | solution.py:36
  11.9 8.2 %collective-permute-start.4 = (bf16[64,512]{1,0:T(8,128)(2,1)S(1)}, bf16[64,512]{1,0:T(8,128)(2,1)S(1)}, u32[]{:S(2)}, u32[]{:S(2)}) collective-permute-start(bf16[64,512]{1,0:T(8,128)(2,1)S(1)} %get-tuple-element.73), channel_id=1, source_target_pairs={{0,5},{1,4},{2,7},{3,6},{4,1},{5,0},{6,3},{7,2},{8,13},{9,12},{10,... | collective-permute-start | bytes 196616 | tf_op jit(solution)/shard_map/ppermute | solution.py:36
  13.1 13.9 %collective-permute-start.7 = (bf16[128,512]{1,0:T(8,128)(2,1)S(1)}, bf16[128,512]{1,0:T(8,128)(2,1)S(1)}, u32[]{:S(2)}, u32[]{:S(2)}) collective-permute-start(bf16[128,512]{1,0:T(8,128)(2,1)S(1)} %get-tuple-element.77), channel_id=1, source_target_pairs={{0,8},{8,0},{16,24},{24,16},{1,9},{9,1},{17,25},{25,17},{2,10},{10... | collective-permute-start | bytes 393224 | tf_op jit(solution)/shard_map/ppermute | solution.py:36
  13.1 13.9 %collective-permute-start.8 = (bf16[128,512]{1,0:T(8,128)(2,1)S(1)}, bf16[128,512]{1,0:T(8,128)(2,1)S(1)}, u32[]{:S(2)}, u32[]{:S(2)}) collective-permute-start(bf16[128,512]{1,0:T(8,128)(2,1)S(1)} %get-tuple-element.78), channel_id=1, source_target_pairs={{0,16},{8,24},{16,0},{24,8},{1,17},{9,25},{17,1},{25,9},{2,18},{10... | collective-permute-start | bytes 393224 | tf_op jit(solution)/shard_map/ppermute | solution.py:36
  14.7 12.3 %collective-permute-start.9 = (bf16[128,512]{1,0:T(8,128)(2,1)S(1)}, bf16[128,512]{1,0:T(8,128)(2,1)S(1)}, u32[]{:S(2)}, u32[]{:S(2)}) collective-permute-start(bf16[128,512]{1,0:T(8,128)(2,1)S(1)} %get-tuple-element.79), channel_id=1, source_target_pairs={{0,24},{8,16},{16,8},{24,0},{1,25},{9,17},{17,9},{25,1},{2,26},{10... | collective-permute-start | bytes 393224 | tf_op jit(solution)/shard_map/ppermute | solution.py:36
  15.7 7.7 %collective-permute-start.5 = (bf16[64,512]{1,0:T(8,128)(2,1)S(1)}, bf16[64,512]{1,0:T(8,128)(2,1)S(1)}, u32[]{:S(2)}, u32[]{:S(2)}) collective-permute-start(bf16[64,512]{1,0:T(8,128)(2,1)S(1)} %get-tuple-element.74), channel_id=1, source_target_pairs={{0,6},{1,7},{2,4},{3,5},{4,2},{5,3},{6,0},{7,1},{8,14},{9,15},{10,... | collective-permute-start | bytes 196616 | tf_op jit(solution)/shard_map/ppermute | solution.py:36
  20.0 7.0 %collective-permute-start.6 = (bf16[64,512]{1,0:T(8,128)(2,1)S(1)}, bf16[64,512]{1,0:T(8,128)(2,1)S(1)}, u32[]{:S(2)}, u32[]{:S(2)}) collective-permute-start(bf16[64,512]{1,0:T(8,128)(2,1)S(1)} %get-tuple-element.75), channel_id=1, source_target_pairs={{0,7},{1,6},{2,5},{3,4},{4,3},{5,2},{6,1},{7,0},{8,15},{9,14},{10,... | collective-permute-start | bytes 196616 | tf_op jit(solution)/shard_map/ppermute | solution.py:36
  29.4 9.7 %collective-permute-start.13 = (bf16[256,128]{1,0:T(8,128)(2,1)S(1)}, bf16[256,128]{1,0:T(8,128)(2,1)S(1)}, u32[]{:S(2)}, u32[]{:S(2)}) collective-permute-start(bf16[256,128]{1,0:T(8,128)(2,1)S(1)} %get-tuple-element.92), channel_id=1, source_target_pairs={{0,16},{8,24},{16,0},{24,8},{1,17},{9,25},{17,1},{25,9},{2,18},{10... | collective-permute-start | bytes 196616 | tf_op jit(solution)/shard_map/ppermute | solution.py:36
  31.0 4.8 %collective-permute-start.10 = (bf16[128,128]{1,0:T(8,128)(2,1)S(1)}, bf16[128,128]{1,0:T(8,128)(2,1)S(1)}, u32[]{:S(2)}, u32[]{:S(2)}) collective-permute-start(bf16[128,128]{1,0:T(8,128)(2,1)S(1)} %get-tuple-element.87), channel_id=1, source_target_pairs={{0,2},{1,3},{2,0},{3,1},{4,6},{5,7},{6,4},{7,5},{8,10},{9,11},{10,... | collective-permute-start | bytes 98312 | tf_op jit(solution)/shard_map/ppermute | solution.py:36
  31.0 5.2 %collective-permute-start.11 = (bf16[128,128]{1,0:T(8,128)(2,1)S(1)}, bf16[128,128]{1,0:T(8,128)(2,1)S(1)}, u32[]{:S(2)}, u32[]{:S(2)}) collective-permute-start(bf16[128,128]{1,0:T(8,128)(2,1)S(1)} %get-tuple-element.88), channel_id=1, source_target_pairs={{0,4},{1,5},{2,6},{3,7},{4,0},{5,1},{6,2},{7,3},{8,12},{9,13},{10,... | collective-permute-start | bytes 98312 | tf_op jit(solution)/shard_map/ppermute | solution.py:36
  33.4 5.7 %collective-permute-start.12 = (bf16[128,128]{1,0:T(8,128)(2,1)S(1)}, bf16[128,128]{1,0:T(8,128)(2,1)S(1)}, u32[]{:S(2)}, u32[]{:S(2)}) collective-permute-start(bf16[128,128]{1,0:T(8,128)(2,1)S(1)} %get-tuple-element.89), channel_id=1, source_target_pairs={{0,6},{1,7},{2,4},{3,5},{4,2},{5,3},{6,0},{7,1},{8,14},{9,15},{10,... | collective-permute-start | bytes 98312 | tf_op jit(solution)/shard_map/ppermute | solution.py:36
  39.1 4.3 %collective-permute-start.14 = (bf16[256,128]{1,0:T(8,128)(2,1)S(1)}, bf16[256,128]{1,0:T(8,128)(2,1)S(1)}, u32[]{:S(2)}, u32[]{:S(2)}) collective-permute-start(bf16[256,128]{1,0:T(8,128)(2,1)S(1)} %get-tuple-element.93), channel_id=1, source_target_pairs={{0,1},{1,0},{2,3},{3,2},{4,5},{5,4},{6,7},{7,6},{8,9},{9,8},{10,11... | collective-permute-start | bytes 196616 | tf_op jit(solution)/shard_map/ppermute | solution.py:36
  39.7 3.7 %collective-permute-start.15 = (bf16[256,128]{1,0:T(8,128)(2,1)S(1)}, bf16[256,128]{1,0:T(8,128)(2,1)S(1)}, u32[]{:S(2)}, u32[]{:S(2)}) collective-permute-start(bf16[256,128]{1,0:T(8,128)(2,1)S(1)} %get-tuple-element.95), channel_id=1, source_target_pairs={{0,8},{8,0},{16,24},{24,16},{1,9},{9,1},{17,25},{25,17},{2,10},{10... | collective-permute-start | bytes 196616 | tf_op jit(solution)/shard_map/ppermute | solution.py:36
where the time goes:
time: 45.4 us; the launch traced here: 45.2 us
  starting transfers between devices  23.5 us (52%)
  Pallas kernels  10.6 us (23%)
  waiting for transfers between devices  9.79 us (22%)
  between operations  1.37 us (3%)
    ppermute x16, starting transfers between devices, permute(): lax.ppermute(x, self.name, [(j, self.partner(j, step)) for j in range(sel...  23.5 us
    pallas_call x7, Pallas kernels, call(): pl.pallas_call(kernel, out_shape=tuple(outs), in_specs=specs, out_specs=t...  10.6 us
    ppermute x16, waiting for transfers between devices, permute(): lax.ppermute(x, self.name, [(j, self.partner(j, step)) for j in range(sel...  9.79 us
  transfers between devices with their start and end apart: 16, of which 4 were waited for; matrix products, arithmetic and copies ran while one was open for 0% of the time, Pallas kernels for 6%

commit v1 on v0

--- a/solution.py
+++ b/solution.py
@@ -36,6 +36,36 @@
         return lax.ppermute(x, self.name, [(j, self.partner(j, step)) for j in range(self.size)])
 
 
+class Route:
+    def __init__(self, axis, m, straight):
+        self.axis, self.m = axis, m
+        through = [s for s in range(axis.outer) if s not in straight] if axis.inner > 1 else []
+        self.relayed = [s for s in through if s > 0]
+        self.passing = int(0 in through)
+        self.on = len(through)
+        self.sends = []
+        for s in range(axis.outer):
+            if s in self.relayed:
+                self.sends.append((s * axis.inner, axis.inner))
+            else:
+                first = 1 + self.passing if s == 0 else 0
+                self.sends += [(s * axis.inner + t, 1) for t in range(first, axis.inner)]
+        self.parts = 1 + len(self.sends) + (self.on > 0)
+
+    def sizes(self):
+        return [self.m] * (1 + self.passing) + [n * self.m for _, n in self.sends]
+
+    def pieces(self):
+        yield 0, 0, 0
+        for i, (step, _) in enumerate(self.sends):
+            yield step, 1 + i, 0
+        for j, s in enumerate([0] * self.passing + self.relayed):
+            yield s * self.axis.inner + 1, self.parts - 1, j * self.m
+
+    def through(self):
+        return [i for i, (_, n) in enumerate(self.sends) if n > 1]
+
+
 def mm(a, b):
     return jnp.dot(a, b, preferred_element_type=F32)
 
@@ -87,14 +117,13 @@
         yield column(ids).astype(jnp.int32)
 
 
-def encode_kernel(axes, n_staged, chunks, *refs):
-    dom, grp = axes
+def encode_kernel(routes, n_staged, chunks, *refs):
     hidden_h, weight_h, send_h, cross_h = refs[:4]
     staged_h = refs[4 : 4 + n_staged]
     outs = refs[4 + n_staged : -4]
     hidden, weight, picks, sems = refs[-4:]
     encoded, send_rows, cross_rows = outs[:3]
-    n = dom.size + grp.size - 2
+    n = sum(len(route.sizes()) - 1 for route in routes)
     sends, staged = outs[3 : 3 + n], outs[3 + n :]
     rows = hidden.shape[0]
     spans = [pl.ds(i * (rows // chunks), rows // chunks) for i in range(chunks)]
@@ -103,9 +132,9 @@
     made = start_copies(pairs, sems)
     later = start_copies(list(zip(staged_h, staged)), sems, len(pairs))
     at = 0
-    for axis, listing, copy in ((dom, send_rows, made[0]), (grp, cross_rows, made[1])):
+    for route, listing, copy in zip(routes, (send_rows, cross_rows), made):
         copy.wait()
-        for ids in slot_ids(axis, listing, range(1, axis.size)):
+        for ids in slot_ids(route.axis, listing, range(1, route.axis.size)):
             picks[at : at + ids.shape[0], :] = one_hot(ids, rows)
             at += ids.shape[0]
     made[2].wait()
@@ -132,7 +161,7 @@
         total[span(dst[0, t], blk), :] += parts[t]
 
 
-def local_kernel(axes, encoded, tiles, src_v, dst_v, bias, remask, send_rows, cross_rows, count, *refs):
+def local_kernel(routes, encoded, tiles, src_v, dst_v, bias, remask, send_rows, cross_rows, count, *refs):
     total, folded, upper, masked, *stay = refs[:-4]
     parts, src, dst, sems = refs[-4:]
     made = start_copies([(src_v, src), (dst_v, dst)], sems)
@@ -141,8 +170,8 @@
     half = folded.shape[1]
     total[...] = jnp.broadcast_to(bias[...], total.shape)
     at = 0
-    for axis, listing, out in zip(axes, (send_rows, cross_rows), stay):
-        for step, ids in enumerate(slot_ids(axis, listing, range(axis.size))):
+    for route, listing, out in zip(routes, (send_rows, cross_rows), stay):
+        for step, ids in enumerate(slot_ids(route.axis, listing, range(route.axis.size))):
             m = ids.shape[0]
             over = ids >= half
             folded[at : at + m, :] = one_hot(jnp.where(over, ids - half, ids), half)
@@ -157,44 +186,49 @@
     add_tiles(total, parts, encoded, tiles, src, dst, count)
 
 
-def latent_kernel(axes, total, tiles, src_v, dst_v, folded, upper, masked, slope, token, weight, *rest):
-    dom, grp = axes
-    n = dom.size + grp.size
-    got, outs = rest[:n], rest[n:-6]
-    summed, pool, parts, src, dst, sems = rest[-6:]
+def fill_pool(routes, parts, pool):
+    at, first = 0, 0
+    for route in routes:
+        axis, m = route.axis, route.m
+        me = lax.axis_index(axis.name)
+        for step, part, row in route.pieces():
+            start = at + axis.partner(me, step, back=True) * m
+            pool[pl.ds(pl.multiple_of(start, m), m), :] = parts[first + part][row : row + m, :]
+        at += axis.size * m
+        first += route.parts
+
+
+def latent_kernel(wide, thin, total, tiles, src_v, dst_v, folded, upper, masked, slope, token, weight, *rest):
+    n = sum(route.parts for route in wide)
+    got, outs, (pool, parts, src, dst, sems) = rest[:n], rest[n:-5], rest[-5:]
+    summed, narrowed = outs[:2]
     made = start_copies([(src_v, src), (dst_v, dst)], sems)
-    at = 0
-    for axis, mine in ((dom, got[: dom.size]), (grp, got[dom.size :])):
-        me = lax.axis_index(axis.name)
-        m = mine[0].shape[0]
-        for step, part in enumerate(mine):
-            start = at + axis.partner(me, step, back=True) * m
-            pool[pl.ds(pl.multiple_of(start, m), m), :] = part[...]
-        at += axis.size * m
-    summed[...] = total[...]
+    fill_pool(wide, got, pool)
     shared = jnp.broadcast_to(token[...].reshape(1, -1).astype(F32), (16, token.shape[0])).astype(BF16)
     replaced = mm(shared, weight[...])[0:1, :]
     wait_copies(made)
     add_tiles(summed, parts, pool, tiles, src, dst)
-    narrowed = outs[0]
     latent = jnp.maximum(summed[...], slope[...] * summed[...]).astype(BF16)
     narrowed[...] = jnp.where(masked[...] > 0, replaced, mm(latent, weight[...])).astype(BF16)
     half, narrow = folded.shape[1], narrowed.shape[1]
     both = jnp.concatenate([narrowed[:half, :], narrowed[half:, :]], axis=1)
     pair = mm(folded[...], both)
     sent = jnp.where(upper[...] > 0, pair[:, narrow:], pair[:, :narrow]).astype(BF16)
-    at, out = 0, 1
-    for axis, mine in ((dom, got[: dom.size]), (grp, got[dom.size :])):
-        m = mine[0].shape[0]
-        for size in [m] * axis.inner + [axis.inner * m] * (axis.outer - 1):
-            outs[out][...] = sent[at : at + size, :]
-            at, out = at + size, out + 1
-
-
-def narrow_local_kernel(narrowed, tiles, src_v, dst_v, bias, count, total, parts, src, dst, sems):
-    made = start_copies([(src_v, src), (dst_v, dst)], sems)
+    at = 0
+    for out, size in zip(outs[2:], [size for route in thin for size in route.sizes()]):
+        out[...] = sent[at : at + size, :]
+        at += size
+
+
+def narrow_local_kernel(narrowed, tiles, src_v, dst_v, halo_tiles, halo_src_v, halo_dst_v, bias, count, total, halo, *refs):
+    parts, src, dst, halo_src, halo_dst, sems = refs
+    made = start_copies([(src_v, src), (dst_v, dst), (halo_src_v, halo_src), (halo_dst_v, halo_dst)], sems)
     total[...] = jnp.broadcast_to(bias[...], total.shape)
+    halo[...] = jnp.zeros(halo.shape, BF16)
     wait_copies(made)
+    n, blk = halo_tiles.shape[:2]
+    for t in range(n):
+        halo[span(halo_dst[0, t], blk), span(halo_src[0, t], blk)] = halo_tiles[t]
     add_tiles(total, parts, narrowed, tiles, src, dst, count)
 
 
@@ -206,39 +240,21 @@
         wanted[n : n + 1, :] = as_row(listed(nodes[...], n * blk, blk))
 
 
-def forward_kernel(axes, *refs):
+def forward_kernel(routes, *refs):
     at = 0
-    outs = refs[sum(axis.outer for axis in axes) :]
-    for axis, out in zip(axes, outs):
-        m = refs[at].shape[0]
-        out[0:m, :] = refs[at][...]
-        for outer in range(1, axis.outer):
-            out[outer * m : (outer + 1) * m, :] = refs[at + outer][m : 2 * m, :]
-        at += axis.outer
-
-
-def final_kernel(axes, total, tiles, src_v, dst_v, targets, scale, wanted, *rest):
-    rebuilt, error, summed, pool, parts, src, dst, sems = rest[-8:]
-    made = start_copies([(src_v, src), (dst_v, dst)], sems)
-    blk = tiles.shape[1]
-    at, ref = 0, 0
-    for axis in axes:
-        me = lax.axis_index(axis.name)
-        stay, outer_got = rest[ref], rest[ref + 1 : ref + axis.outer]
-        ref += axis.outer
-        m = stay.shape[0]
-        pieces = [(0, stay, 0)]
-        pieces += [((1 + i) * axis.inner, got, 0) for i, got in enumerate(outer_got)]
-        if axis.inner > 1:
-            pieces += [(i * axis.inner + 1, rest[ref], i * m) for i in range(axis.outer)]
-            ref += 1
-        for step, got, where in pieces:
-            start = at + axis.partner(me, step, back=True) * m
-            pool[pl.ds(pl.multiple_of(start, m), m), :] = got[where : where + m, :]
-        at += axis.size * m
-    summed[...] = total[...]
-    wait_copies(made)
-    add_tiles(summed, parts, pool, tiles, src, dst)
+    outs = refs[sum(route.on for route in routes) :]
+    for route, out in zip(routes, outs):
+        m = route.m
+        for j in range(route.on):
+            first = 0 if j < route.passing else m
+            out[j * m : (j + 1) * m, :] = refs[at + j][first : first + m, :]
+        at += route.on
+
+
+def final_kernel(routes, blk, total, halo, targets, scale, wanted, *rest):
+    rebuilt, error, pool = rest[-3:]
+    fill_pool(routes, rest, pool)
+    summed = total[...] + mm(halo[...], pool[...])
     for b in range(scale.shape[0]):
         rounded = summed[b * blk : (b + 1) * blk, :].astype(BF16)
         rebuilt[b * blk : (b + 1) * blk, :] = rounded
@@ -250,16 +266,45 @@
         error[b : b + 1, :] = jnp.where(wanted[b : b + 1, :] > 0, (1.0 - cosine) ** 2, 0.0)
 
 
-def call(kernel, outs, specs, args, scratch=(), flops=10**9):
+def call(kernel, outs, specs, args, scratch=(), flops=10**9, aliases=None):
     return pl.pallas_call(
         kernel,
         out_shape=tuple(outs),
         in_specs=specs,
         out_specs=tuple(VMEM for _ in outs),
         scratch_shapes=scratch,
+        input_output_aliases=aliases or {},
         compiler_params=pltpu.CompilerParams(vmem_limit_bytes=GRANT),
         cost_estimate=pl.CostEstimate(flops=flops, bytes_accessed=2**20, transcendentals=0),
     )(*args)
+
+
+def send_out(routes, sends):
+    passing, came = [], []
+    for route in routes:
+        n = route.passing
+        passing.append(sends[:n])
+        out, sends = sends[n : n + len(route.sends)], sends[n + len(route.sends) :]
+        came.append([route.axis.permute(x, step) for x, (step, _) in zip(out, route.sends)])
+    return passing, came
+
+
+def send_on(routes, passing, came):
+    on = [i for i, route in enumerate(routes) if route.on]
+    came = [list(x) for x in came]
+    if on:
+        args = [x for i in on for x in (*passing[i], *(came[i][j] for j in routes[i].through()))]
+        width = args[0].shape[1]
+        blocks = call(
+            functools.partial(forward_kernel, [routes[i] for i in on]),
+            [jax.ShapeDtypeStruct((routes[i].on * routes[i].m, width), BF16) for i in on],
+            [VMEM] * len(args),
+            args,
+            flops=10**7,
+        )
+        for i, x in zip(on, blocks):
+            came[i].append(routes[i].axis.permute(x, 1))
+    return came
 
 
 def per_device(
@@ -294,7 +339,6 @@
     blocks = rows // blk
     m_dom, m_grp = send_rows.shape[1], cross_rows.shape[1]
     halo_rows = n_dom * m_dom + n_grp * m_grp
-    dom, grp = axes = (Axis("dom", n_dom), Axis("group", n_grp))
     chunks = 4
     to_stage = (
         local_tiles,
@@ -320,9 +364,10 @@
         return [pltpu.SMEM(x.shape, i32) for x in arrays] + [pltpu.SemaphoreType.DMA((len(arrays),))]
 
     fed = [pltpu.with_memory_space_constraint(x, pltpu.HBM) for x in (hidden, enc_weight, send_rows, cross_rows, *to_stage)]
-    slots = [sds((m_dom, width), BF16)] * (n_dom - 1) + [sds((m_grp, width), BF16)] * (n_grp - 1)
+    wide, thin = routes(n_dom, n_grp, m_dom, m_grp)
+    slots = [sds((size, width), BF16) for route in wide for size in route.sizes()[1:]]
     encoded, send_rows, cross_rows, *outs = call(
-        functools.partial(encode_kernel, axes, len(to_stage), chunks),
+        functools.partial(encode_kernel, wide, len(to_stage), chunks),
         [sds((rows, width), BF16)] + like((send_rows, cross_rows)) + slots + like(to_stage),
         [HBM] * len(fed),
         fed,
@@ -336,11 +381,9 @@
     sends, staged = outs[: len(slots)], outs[len(slots) :]
     tiles, src, dst, halo_edges, halo_from, halo_to = staged[:6]
     enc_bias, enc_slope, dec_token, dec_weight, dec_bias, targets, mask_nodes, remask_nodes = staged[6:]
-    dom_got = [dom.permute(sends[s - 1], s) for s in range(1, n_dom)]
-    grp_got = [grp.permute(sends[n_dom + s - 2], s) for s in range(1, n_grp)]
-
-    total, folded, upper, masked, dom_stay, grp_stay = call(
-        functools.partial(local_kernel, axes),
+    passing, came = send_out(wide, sends)
+    total, folded, upper, masked, *stay = call(
+        functools.partial(local_kernel, wide),
         [
             sds((rows, width), F32),
             sds((halo_rows, rows // 2), BF16),
@@ -353,32 +396,26 @@
         (encoded, tiles, src, dst, enc_bias, remask_nodes, send_rows, cross_rows, local_count),
         [pltpu.VMEM((n_tiles, blk, width), F32)] + scalars(src, dst),
     )
-    slots = []
-    for axis, m in ((dom, m_dom), (grp, m_grp)):
-        slots += [sds((m, narrow), BF16)] * axis.inner
-        slots += [sds((axis.inner * m, narrow), BF16)] * (axis.outer - 1)
+    came = send_on(wide, passing, came)
     args = (total, halo_edges, halo_from, halo_to, folded, upper, masked, enc_slope, dec_token, dec_weight)
-    args += (dom_stay, *dom_got, grp_stay, *grp_got)
-    narrowed, *outs = call(
-        functools.partial(latent_kernel, axes),
-        [sds((rows, narrow), BF16)] + slots,
+    args += (stay[0], *came[0], stay[1], *came[1])
+    _, narrowed, *outs = call(
+        functools.partial(latent_kernel, wide, thin),
+        [sds((rows, width), F32), sds((rows, narrow), BF16)] + [sds((size, narrow), BF16) for route in thin for size in route.sizes()],
         [VMEM] * len(args),
         args,
-        [pltpu.VMEM((rows, width), F32), pltpu.VMEM((halo_rows, width), BF16), pltpu.VMEM((n_halo, blk, width), F32)]
-        + scalars(halo_from, halo_to),
-    )
-    stay, passing, outer_got = [], [], []
-    for axis in axes:
-        stay.append(outs[0])
-        passing.append(outs[1 : axis.inner])
-        rest, outs = outs[axis.inner : axis.inner + axis.outer - 1], outs[axis.inner + axis.outer - 1 :]
-        outer_got.append([axis.permute(x, (i + 1) * axis.inner) for i, x in enumerate(rest)])
-    (total,) = call(
+        [pltpu.VMEM((halo_rows, width), BF16), pltpu.VMEM((n_halo, blk, width), F32)] + scalars(halo_from, halo_to),
+        aliases={0: 0},
+    )
+    n = len(thin[0].sizes())
+    stay, outs = [outs[0], outs[n]], outs[1:n] + outs[n + 1 :]
+    passing, came = send_out(thin, outs)
+    total, halo = call(
         narrow_local_kernel,
-        [sds((rows, narrow), F32)],
-        [VMEM] * 5 + [SMEM],
-        (narrowed, tiles, src, dst, dec_bias, local_count),
-        [pltpu.VMEM((n_tiles, blk, narrow), F32)] + scalars(src, dst),
+        [sds((rows, narrow), F32), sds((rows, halo_rows), BF16)],
+        [VMEM] * 8 + [SMEM],
+        (narrowed, tiles, src, dst, halo_edges, halo_from, halo_to, dec_bias, local_count),
+        [pltpu.VMEM((n_tiles, blk, narrow), F32)] + scalars(src, dst, halo_from, halo_to),
     )
     scale, wanted = call(
         functools.partial(target_kernel, blk),
@@ -386,29 +423,23 @@
         [VMEM] * 2,
         (targets, mask_nodes),
     )
-    split = [i for i, axis in enumerate(axes) if axis.inner > 1]
-    inner_got = [[], []]
-    if split:
-        args = [x for i in split for x in (*passing[i], *outer_got[i])]
-        forward = call(
-            functools.partial(forward_kernel, [axes[i] for i in split]),
-            [sds((axes[i].outer * (m_dom, m_grp)[i], narrow), BF16) for i in split],
-            [VMEM] * len(args),
-            args,
-            flops=10**7,
-        )
-        for i, x in zip(split, forward):
-            inner_got[i] = [axes[i].permute(x, 1)]
-    got = [x for i in range(2) for x in (stay[i], *outer_got[i], *inner_got[i])]
+    came = send_on(thin, passing, came)
+    got = (stay[0], *came[0], stay[1], *came[1])
     rebuilt, error = call(
-        functools.partial(final_kernel, axes),
+        functools.partial(final_kernel, thin, blk),
         [sds((rows, narrow), BF16), sds((blocks, blk), F32)],
-        [VMEM] * (7 + len(got)),
-        (total, halo_edges, halo_from, halo_to, targets, scale, wanted, *got),
-        [pltpu.VMEM((rows, narrow), F32), pltpu.VMEM((halo_rows, narrow), BF16), pltpu.VMEM((n_halo, blk, narrow), F32)]
-        + scalars(halo_from, halo_to),
+        [VMEM] * (5 + len(got)),
+        (total, halo, targets, scale, wanted, *got),
+        [pltpu.VMEM((halo_rows, narrow), BF16)],
     )
     return rebuilt, error.reshape(-1)
+
+
+def routes(n_dom, n_grp, m_dom, m_grp):
+    dom, grp = Axis("dom", n_dom), Axis("group", n_grp)
+    wide = [Route(axis, m, range(axis.outer)) for axis, m in ((dom, m_dom), (grp, m_grp))]
+    thin = [Route(axis, m, ()) for axis, m in ((dom, m_dom), (grp, m_grp))]
+    return wide, thin
 
 
 def solution(mesh):

time: 45.4 us -> 45.1 us (level)
  no operation moved by 1% of the time
where the time goes in v1:
time: 45.1 us; the launch traced here: 44.9 us
  starting transfers between devices  23.5 us (52%)
  Pallas kernels  10.4 us (23%)
  waiting for transfers between devices  9.69 us (21%)
  between operations  1.37 us (3%)
    ppermute x16, starting transfers between devices, permute(): lax.ppermute(x, self.name, [(j, self.partner(j, step)) for j in range(sel...  23.5 us
    pallas_call x7, Pallas kernels, call(): pl.pallas_call(kernel, out_shape=tuple(outs), in_specs=specs, out_specs=t...  10.4 us
    ppermute x16, waiting for transfers between devices, permute(): lax.ppermute(x, self.name, [(j, self.partner(j, step)) for j in range(sel...  9.69 us
  transfers between devices with their start and end apart: 16, of which 4 were waited for; matrix products, arithmetic and copies ran while one was open for 0% of the time, Pallas kernels for 6%

profile of v1, /device:TPU:0, one launch (start us, length us, event | category | flops | bytes accessed | tf_op | source)
XLA Modules:
  0.0 44.9 jit_solution(9389178243391325530)
XLA Ops:
  0.6 3.6 %shard_map.194 = (bf16[1024,512]{1,0:T(8,128)(2,1)S(1)}, s32[8,64]{1,0:T(8,128)S(1)}, s32[4,128]{1,0:T(4,128)S(1)}, bf16[64,512]{1,0:T(8,128)(2,1)S(1)}, bf16[64...) custom-call(bf16[1024,512]{1,0:T(8,128)(2,1)} %refs_0_.1, ...), custom_call_target="tpu_custom_call" | custom-call | flops 1000000000 | bytes 1048576 | tf_op jit(solution)/shard_map/pallas_call | solution.py:270
  4.2 3.0 %collective-permute-start = (bf16[64,512]{1,0:T(8,128)(2,1)S(1)}, bf16[64,512]{1,0:T(8,128)(2,1)S(1)}, u32[]{:S(2)}, u32[]{:S(2)}) collective-permute-start(bf16[64,512]{1,0:T(8,128)(2,1)S(1)} %get-tuple-element.71), channel_id=1, source_target_pairs={{0,1},{1,0},{2,3},{3,2},{4,5},{5,4},{6,7},{7,6},{8,9},{9,8},{10,11... | collective-permute-start | bytes 196616 | tf_op jit(solution)/shard_map/ppermute | solution.py:36
  7.3 1.6 %collective-permute-start.1 = (bf16[64,512]{1,0:T(8,128)(2,1)S(1)}, bf16[64,512]{1,0:T(8,128)(2,1)S(1)}, u32[]{:S(2)}, u32[]{:S(2)}) collective-permute-start(bf16[64,512]{1,0:T(8,128)(2,1)S(1)} %get-tuple-element.72), channel_id=1, source_target_pairs={{0,2},{1,3},{2,0},{3,1},{4,6},{5,7},{6,4},{7,5},{8,10},{9,11},{10,... | collective-permute-start | bytes 196616 | tf_op jit(solution)/shard_map/ppermute | solution.py:36
  8.8 0.0 collective-permute-start.2
  8.8 3.0 %collective-permute-start.3 = (bf16[64,512]{1,0:T(8,128)(2,1)S(1)}, bf16[64,512]{1,0:T(8,128)(2,1)S(1)}, u32[]{:S(2)}, u32[]{:S(2)}) collective-permute-start(bf16[64,512]{1,0:T(8,128)(2,1)S(1)} %get-tuple-element.74), channel_id=1, source_target_pairs={{0,4},{1,5},{2,6},{3,7},{4,0},{5,1},{6,2},{7,3},{8,12},{9,13},{10,... | collective-permute-start | bytes 196616 | tf_op jit(solution)/shard_map/ppermute | solution.py:36
  11.9 1.3 %collective-permute-start.4 = (bf16[64,512]{1,0:T(8,128)(2,1)S(1)}, bf16[64,512]{1,0:T(8,128)(2,1)S(1)}, u32[]{:S(2)}, u32[]{:S(2)}) collective-permute-start(bf16[64,512]{1,0:T(8,128)(2,1)S(1)} %get-tuple-element.75), channel_id=1, source_target_pairs={{0,5},{1,4},{2,7},{3,6},{4,1},{5,0},{6,3},{7,2},{8,13},{9,12},{10,... | collective-permute-start | bytes 196616 | tf_op jit(solution)/shard_map/ppermute | solution.py:36
  13.1 0.0 collective-permute-done.rest_1_
  13.1 0.0 collective-permute-start.7
  13.1 0.0 collective-permute-done.1.rest_2_
  13.1 1.6 %collective-permute-start.8 = (bf16[128,512]{1,0:T(8,128)(2,1)S(1)}, bf16[128,512]{1,0:T(8,128)(2,1)S(1)}, u32[]{:S(2)}, u32[]{:S(2)}) collective-permute-start(bf16[128,512]{1,0:T(8,128)(2,1)S(1)} %get-tuple-element.80), channel_id=1, source_target_pairs={{0,16},{8,24},{16,0},{24,8},{1,17},{9,25},{17,1},{25,9},{2,18},{10... | collective-permute-start | bytes 393224 | tf_op jit(solution)/shard_map/ppermute | solution.py:36
  14.7 0.3 collective-permute-start.9
  15.6 0.0 collective-permute-done.3.rest_4_
  15.7 4.4 %collective-permute-start.5 = (bf16[64,512]{1,0:T(8,128)(2,1)S(1)}, bf16[64,512]{1,0:T(8,128)(2,1)S(1)}, u32[]{:S(2)}, u32[]{:S(2)}) collective-permute-start(bf16[64,512]{1,0:T(8,128)(2,1)S(1)} %get-tuple-element.76), channel_id=1, source_target_pairs={{0,6},{1,7},{2,4},{3,5},{4,2},{5,3},{6,0},{7,1},{8,14},{9,15},{10,... | collective-permute-start | bytes 196616 | tf_op jit(solution)/shard_map/ppermute | solution.py:36
  20.0 0.0 collective-permute-done.4.rest_5_
  20.0 1.8 %collective-permute-start.6 = (bf16[64,512]{1,0:T(8,128)(2,1)S(1)}, bf16[64,512]{1,0:T(8,128)(2,1)S(1)}, u32[]{:S(2)}, u32[]{:S(2)}) collective-permute-start(bf16[64,512]{1,0:T(8,128)(2,1)S(1)} %get-tuple-element.77), channel_id=1, source_target_pairs={{0,7},{1,6},{2,5},{3,4},{4,3},{5,2},{6,1},{7,0},{8,15},{9,14},{10,... | collective-permute-start | bytes 196616 | tf_op jit(solution)/shard_map/ppermute | solution.py:36
  21.8 1.5 %shard_map.195 = (f32[1024,512]{1,0:T(8,128)S(1)}, bf16[1024,512]{1,0:T(8,128)(2,1)S(1)}, f32[1024,128]{1,0:T(8,128)S(1)}, f32[1024,128]{1,0:T(8,128)S(1)}, bf16...) custom-call(bf16[1024,512]{1,0:T(8,128)(2,1)S(1)} %get-tuple-element.52.encoded, ...), custom_call_target="tpu_custom_call" | custom-call | flops 1000000000 | bytes 1048576 | tf_op jit(solution)/shard_map/pallas_call | solution.py:270
  23.4 0.0 collective-permute-done.5.rest_6_
  23.4 3.6 %collective-permute-done.6.rest_7_ = bf16[64,512]{1,0:T(8,128)(2,1)S(1)} collective-permute-done((bf16[64,512]{1,0:T(8,128)(2,1)S(1)}, bf16[64,512]{1,0:T(8,128)(2,1)S(1)}, u32[]{:S(2)}, u32[]{:S(2)}) %collective-permute-start.6) | collective-permute-done | bytes 65568 | tf_op jit(solution)/shard_map/ppermute | solution.py:36
  27.0 0.0 collective-permute-done.7.rest_9_
  27.0 0.0 collective-permute-done.8.rest_10_
  27.0 0.0 collective-permute-done.9.rest_11_
  27.0 2.4 %shard_map.196 = (f32[1024,512]{1,0:T(8,128)S(1)}, bf16[1024,128]{1,0:T(8,128)(2,1)S(1)}, bf16[64,128]{1,0:T(8,128)(2,1)S(1)}, bf16[64,128]{1,0:T(8,128)(2,1)S(1...) custom-call(f32[1024,512]{1,0:T(8,128)S(1)} %get-tuple-element.60.to, ...), custom_call_target="tpu_custom_call", output_to_operand_aliasing={{0}: (0, {})} | custom-call | flops 1000000000 | bytes 1048576 | tf_op jit(solution)/shard_map/pallas_call | solution.py:270
  29.4 1.6 %collective-permute-start.13 = (bf16[256,128]{1,0:T(8,128)(2,1)S(1)}, bf16[256,128]{1,0:T(8,128)(2,1)S(1)}, u32[]{:S(2)}, u32[]{:S(2)}) collective-permute-start(bf16[256,128]{1,0:T(8,128)(2,1)S(1)} %get-tuple-element.96), channel_id=1, source_target_pairs={{0,16},{8,24},{16,0},{24,8},{1,17},{9,25},{17,1},{25,9},{2,18},{10... | collective-permute-start | bytes 196616 | tf_op jit(solution)/shard_map/ppermute | solution.py:36
  31.0 2.4 %collective-permute-start.11 = (bf16[128,128]{1,0:T(8,128)(2,1)S(1)}, bf16[128,128]{1,0:T(8,128)(2,1)S(1)}, u32[]{:S(2)}, u32[]{:S(2)}) collective-permute-start(bf16[128,128]{1,0:T(8,128)(2,1)S(1)} %get-tuple-element.92), channel_id=1, source_target_pairs={{0,4},{1,5},{2,6},{3,7},{4,0},{5,1},{6,2},{7,3},{8,12},{9,13},{10,... | collective-permute-start | bytes 98312 | tf_op jit(solution)/shard_map/ppermute | solution.py:36
  33.4 2.0 %collective-permute-start.12 = (bf16[128,128]{1,0:T(8,128)(2,1)S(1)}, bf16[128,128]{1,0:T(8,128)(2,1)S(1)}, u32[]{:S(2)}, u32[]{:S(2)}) collective-permute-start(bf16[128,128]{1,0:T(8,128)(2,1)S(1)} %get-tuple-element.93), channel_id=1, source_target_pairs={{0,6},{1,7},{2,4},{3,5},{4,2},{5,3},{6,0},{7,1},{8,14},{9,15},{10,... | collective-permute-start | bytes 98312 | tf_op jit(solution)/shard_map/ppermute | solution.py:36
  35.4 0.4 shard_map.198
  35.8 0.4 collective-permute-done.11.refs_2_.rest_2_
  36.2 2.9 %collective-permute-done.12.refs_3_.rest_3_ = bf16[128,128]{1,0:T(8,128)(2,1)S(1)} collective-permute-done((bf16[128,128]{1,0:T(8,128)(2,1)S(1)}, bf16[128,128]{1,0:T(8,128)(2,1)S(1)}, u32[]{:S(2)}, u32[]{:S(2)}) %collective-permute-start.12) | collective-permute-done | bytes 32800 | tf_op jit(solution)/shard_map/ppermute | solution.py:36
  39.1 0.6 %collective-permute-start.14 = (bf16[256,128]{1,0:T(8,128)(2,1)S(1)}, bf16[256,128]{1,0:T(8,128)(2,1)S(1)}, u32[]{:S(2)}, u32[]{:S(2)}) collective-permute-start(bf16[256,128]{1,0:T(8,128)(2,1)S(1)} %get-tuple-element.97), channel_id=1, source_target_pairs={{0,1},{1,0},{2,3},{3,2},{4,5},{5,4},{6,7},{7,6},{8,9},{9,8},{10,11... | collective-permute-start | bytes 196616 | tf_op jit(solution)/shard_map/ppermute | solution.py:36
  39.7 1.0 %shard_map.197 = (f32[1024,128]{1,0:T(8,128)S(1)}, bf16[1024,1024]{1,0:T(8,128)(2,1)S(1)}) custom-call(bf16[1024,128]{1,0:T(8,128)(2,1)S(1)} %get-tuple-element.82.narrowed, bf16[12,128,128]{2,1,0:T(8,128)(2,1)S(1)} %get-tuple-element.53.tiles, s32[1,12]{1,0:T(1,128)S(1)} %get-tuple-element.54.src_v, s32[1,12]{1,0:T(1,128)S(1)} %get-tuple-element.55.dst_v, ...), custom_call_target="tpu_custom_call" | custom-call | flops 1000000000 | bytes 1048576 | tf_op jit(solution)/shard_map/pallas_call | solution.py:270
  40.7 2.8 %collective-permute-done.14.rest_4_ = bf16[256,128]{1,0:T(8,128)(2,1)S(1)} collective-permute-done((bf16[256,128]{1,0:T(8,128)(2,1)S(1)}, bf16[256,128]{1,0:T(8,128)(2,1)S(1)}, u32[]{:S(2)}, u32[]{:S(2)}) %collective-permute-start.14) | collective-permute-done | bytes 65568 | tf_op jit(solution)/shard_map/ppermute | solution.py:36
  43.4 1.5 %shard_map.200 = (bf16[1024,128]{1,0:T(8,128)(2,1)}, f32[8,128]{1,0:T(8,128)}) custom-call(f32[1024,128]{1,0:T(8,128)S(1)} %get-tuple-element.84.total, bf16[1024,1024]{1,0:T(8,128)(2,1)S(1)} %get-tuple-element.85.halo, bf16[1024,128]{1,0:T(8,128)(2,1)S(1)} %get-tuple-element.86.targets, f32[8,128]{1,0:T(8,128)S(1)} %get-tuple-element.88.scale, ...), custom_call_target="tpu_custom_call" | custom-call | flops 1000000000 | bytes 1048576 | tf_op jit(solution)/shard_map/pallas_call | solution.py:270
  (7 shorter events, 0.0 us)
Async XLA Ops:
  4.2 8.9 %collective-permute-start = (bf16[64,512]{1,0:T(8,128)(2,1)S(1)}, bf16[64,512]{1,0:T(8,128)(2,1)S(1)}, u32[]{:S(2)}, u32[]{:S(2)}) collective-permute-start(bf16[64,512]{1,0:T(8,128)(2,1)S(1)} %get-tuple-element.71), channel_id=1, source_target_pairs={{0,1},{1,0},{2,3},{3,2},{4,5},{5,4},{6,7},{7,6},{8,9},{9,8},{10,11... | collective-permute-start | bytes 196616 | tf_op jit(solution)/shard_map/ppermute | solution.py:36
  7.3 5.9 %collective-permute-start.1 = (bf16[64,512]{1,0:T(8,128)(2,1)S(1)}, bf16[64,512]{1,0:T(8,128)(2,1)S(1)}, u32[]{:S(2)}, u32[]{:S(2)}) collective-permute-start(bf16[64,512]{1,0:T(8,128)(2,1)S(1)} %get-tuple-element.72), channel_id=1, source_target_pairs={{0,2},{1,3},{2,0},{3,1},{4,6},{5,7},{6,4},{7,5},{8,10},{9,11},{10,... | collective-permute-start | bytes 196616 | tf_op jit(solution)/shard_map/ppermute | solution.py:36
  8.8 5.9 %collective-permute-start.2 = (bf16[64,512]{1,0:T(8,128)(2,1)S(1)}, bf16[64,512]{1,0:T(8,128)(2,1)S(1)}, u32[]{:S(2)}, u32[]{:S(2)}) collective-permute-start(bf16[64,512]{1,0:T(8,128)(2,1)S(1)} %get-tuple-element.73), channel_id=1, source_target_pairs={{0,3},{1,2},{2,1},{3,0},{4,7},{5,6},{6,5},{7,4},{8,11},{9,10},{10,... | collective-permute-start | bytes 196616 | tf_op jit(solution)/shard_map/ppermute | solution.py:36
  8.8 6.8 %collective-permute-start.3 = (bf16[64,512]{1,0:T(8,128)(2,1)S(1)}, bf16[64,512]{1,0:T(8,128)(2,1)S(1)}, u32[]{:S(2)}, u32[]{:S(2)}) collective-permute-start(bf16[64,512]{1,0:T(8,128)(2,1)S(1)} %get-tuple-element.74), channel_id=1, source_target_pairs={{0,4},{1,5},{2,6},{3,7},{4,0},{5,1},{6,2},{7,3},{8,12},{9,13},{10,... | collective-permute-start | bytes 196616 | tf_op jit(solution)/shard_map/ppermute | solution.py:36
  11.9 8.2 %collective-permute-start.4 = (bf16[64,512]{1,0:T(8,128)(2,1)S(1)}, bf16[64,512]{1,0:T(8,128)(2,1)S(1)}, u32[]{:S(2)}, u32[]{:S(2)}) collective-permute-start(bf16[64,512]{1,0:T(8,128)(2,1)S(1)} %get-tuple-element.75), channel_id=1, source_target_pairs={{0,5},{1,4},{2,7},{3,6},{4,1},{5,0},{6,3},{7,2},{8,13},{9,12},{10,... | collective-permute-start | bytes 196616 | tf_op jit(solution)/shard_map/ppermute | solution.py:36
  13.1 13.9 %collective-permute-start.7 = (bf16[128,512]{1,0:T(8,128)(2,1)S(1)}, bf16[128,512]{1,0:T(8,128)(2,1)S(1)}, u32[]{:S(2)}, u32[]{:S(2)}) collective-permute-start(bf16[128,512]{1,0:T(8,128)(2,1)S(1)} %get-tuple-element.79), channel_id=1, source_target_pairs={{0,8},{8,0},{16,24},{24,16},{1,9},{9,1},{17,25},{25,17},{2,10},{10... | collective-permute-start | bytes 393224 | tf_op jit(solution)/shard_map/ppermute | solution.py:36
  13.1 13.9 %collective-permute-start.8 = (bf16[128,512]{1,0:T(8,128)(2,1)S(1)}, bf16[128,512]{1,0:T(8,128)(2,1)S(1)}, u32[]{:S(2)}, u32[]{:S(2)}) collective-permute-start(bf16[128,512]{1,0:T(8,128)(2,1)S(1)} %get-tuple-element.80), channel_id=1, source_target_pairs={{0,16},{8,24},{16,0},{24,8},{1,17},{9,25},{17,1},{25,9},{2,18},{10... | collective-permute-start | bytes 393224 | tf_op jit(solution)/shard_map/ppermute | solution.py:36
  14.7 12.3 %collective-permute-start.9 = (bf16[128,512]{1,0:T(8,128)(2,1)S(1)}, bf16[128,512]{1,0:T(8,128)(2,1)S(1)}, u32[]{:S(2)}, u32[]{:S(2)}) collective-permute-start(bf16[128,512]{1,0:T(8,128)(2,1)S(1)} %get-tuple-element.81), channel_id=1, source_target_pairs={{0,24},{8,16},{16,8},{24,0},{1,25},{9,17},{17,9},{25,1},{2,26},{10... | collective-permute-start | bytes 393224 | tf_op jit(solution)/shard_map/ppermute | solution.py:36
  15.7 7.7 %collective-permute-start.5 = (bf16[64,512]{1,0:T(8,128)(2,1)S(1)}, bf16[64,512]{1,0:T(8,128)(2,1)S(1)}, u32[]{:S(2)}, u32[]{:S(2)}) collective-permute-start(bf16[64,512]{1,0:T(8,128)(2,1)S(1)} %get-tuple-element.76), channel_id=1, source_target_pairs={{0,6},{1,7},{2,4},{3,5},{4,2},{5,3},{6,0},{7,1},{8,14},{9,15},{10,... | collective-permute-start | bytes 196616 | tf_op jit(solution)/shard_map/ppermute | solution.py:36
  20.0 7.0 %collective-permute-start.6 = (bf16[64,512]{1,0:T(8,128)(2,1)S(1)}, bf16[64,512]{1,0:T(8,128)(2,1)S(1)}, u32[]{:S(2)}, u32[]{:S(2)}) collective-permute-start(bf16[64,512]{1,0:T(8,128)(2,1)S(1)} %get-tuple-element.77), channel_id=1, source_target_pairs={{0,7},{1,6},{2,5},{3,4},{4,3},{5,2},{6,1},{7,0},{8,15},{9,14},{10,... | collective-permute-start | bytes 196616 | tf_op jit(solution)/shard_map/ppermute | solution.py:36
  29.4 9.7 %collective-permute-start.13 = (bf16[256,128]{1,0:T(8,128)(2,1)S(1)}, bf16[256,128]{1,0:T(8,128)(2,1)S(1)}, u32[]{:S(2)}, u32[]{:S(2)}) collective-permute-start(bf16[256,128]{1,0:T(8,128)(2,1)S(1)} %get-tuple-element.96), channel_id=1, source_target_pairs={{0,16},{8,24},{16,0},{24,8},{1,17},{9,25},{17,1},{25,9},{2,18},{10... | collective-permute-start | bytes 196616 | tf_op jit(solution)/shard_map/ppermute | solution.py:36
  31.0 4.8 %collective-permute-start.10 = (bf16[128,128]{1,0:T(8,128)(2,1)S(1)}, bf16[128,128]{1,0:T(8,128)(2,1)S(1)}, u32[]{:S(2)}, u32[]{:S(2)}) collective-permute-start(bf16[128,128]{1,0:T(8,128)(2,1)S(1)} %get-tuple-element.91), channel_id=1, source_target_pairs={{0,2},{1,3},{2,0},{3,1},{4,6},{5,7},{6,4},{7,5},{8,10},{9,11},{10,... | collective-permute-start | bytes 98312 | tf_op jit(solution)/shard_map/ppermute | solution.py:36
  31.0 5.2 %collective-permute-start.11 = (bf16[128,128]{1,0:T(8,128)(2,1)S(1)}, bf16[128,128]{1,0:T(8,128)(2,1)S(1)}, u32[]{:S(2)}, u32[]{:S(2)}) collective-permute-start(bf16[128,128]{1,0:T(8,128)(2,1)S(1)} %get-tuple-element.92), channel_id=1, source_target_pairs={{0,4},{1,5},{2,6},{3,7},{4,0},{5,1},{6,2},{7,3},{8,12},{9,13},{10,... | collective-permute-start | bytes 98312 | tf_op jit(solution)/shard_map/ppermute | solution.py:36
  33.4 5.7 %collective-permute-start.12 = (bf16[128,128]{1,0:T(8,128)(2,1)S(1)}, bf16[128,128]{1,0:T(8,128)(2,1)S(1)}, u32[]{:S(2)}, u32[]{:S(2)}) collective-permute-start(bf16[128,128]{1,0:T(8,128)(2,1)S(1)} %get-tuple-element.93), channel_id=1, source_target_pairs={{0,6},{1,7},{2,4},{3,5},{4,2},{5,3},{6,0},{7,1},{8,14},{9,15},{10,... | collective-permute-start | bytes 98312 | tf_op jit(solution)/shard_map/ppermute | solution.py:36
  39.1 4.3 %collective-permute-start.14 = (bf16[256,128]{1,0:T(8,128)(2,1)S(1)}, bf16[256,128]{1,0:T(8,128)(2,1)S(1)}, u32[]{:S(2)}, u32[]{:S(2)}) collective-permute-start(bf16[256,128]{1,0:T(8,128)(2,1)S(1)} %get-tuple-element.97), channel_id=1, source_target_pairs={{0,1},{1,0},{2,3},{3,2},{4,5},{5,4},{6,7},{7,6},{8,9},{9,8},{10,11... | collective-permute-start | bytes 196616 | tf_op jit(solution)/shard_map/ppermute | solution.py:36
  39.7 3.7 %collective-permute-start.15 = (bf16[256,128]{1,0:T(8,128)(2,1)S(1)}, bf16[256,128]{1,0:T(8,128)(2,1)S(1)}, u32[]{:S(2)}, u32[]{:S(2)}) collective-permute-start(bf16[256,128]{1,0:T(8,128)(2,1)S(1)} %get-tuple-element.99), channel_id=1, source_target_pairs={{0,8},{8,0},{16,24},{24,16},{1,9},{9,1},{17,25},{25,17},{2,10},{10... | collective-permute-start | bytes 196616 | tf_op jit(solution)/shard_map/ppermute | solution.py:36

commit v2 on v1

--- a/solution.py
+++ b/solution.py
@@ -161,10 +161,12 @@
         total[span(dst[0, t], blk), :] += parts[t]
 
 
-def local_kernel(routes, encoded, tiles, src_v, dst_v, bias, remask, send_rows, cross_rows, count, *refs):
-    total, folded, upper, masked, *stay = refs[:-4]
-    parts, src, dst, sems = refs[-4:]
+def local_kernel(routes, n_staged, encoded, tiles, src_v, dst_v, bias, remask, send_rows, cross_rows, count, *refs):
+    staged_h, outs, (parts, src, dst, sems) = refs[:n_staged], refs[n_staged:-4], refs[-4:]
+    total, folded, upper, masked = outs[:4]
+    stay, staged = outs[4 : len(outs) - n_staged], outs[len(outs) - n_staged :]
     made = start_copies([(src_v, src), (dst_v, dst)], sems)
+    later = start_copies(list(zip(staged_h, staged)), sems, len(made))
     blk = tiles.shape[1]
     rows = encoded.shape[0]
     half = folded.shape[1]
@@ -184,6 +186,7 @@
         masked[n * blk : (n + 1) * blk, :] = jnp.broadcast_to(hit, (blk, masked.shape[1]))
     wait_copies(made)
     add_tiles(total, parts, encoded, tiles, src, dst, count)
+    wait_copies(later)
 
 
 def fill_pool(routes, parts, pool):
@@ -208,8 +211,11 @@
     replaced = mm(shared, weight[...])[0:1, :]
     wait_copies(made)
     add_tiles(summed, parts, pool, tiles, src, dst)
-    latent = jnp.maximum(summed[...], slope[...] * summed[...]).astype(BF16)
-    narrowed[...] = jnp.where(masked[...] > 0, replaced, mm(latent, weight[...])).astype(BF16)
+    quarter = summed.shape[0] // 4
+    for i in range(4):
+        s = pl.ds(i * quarter, quarter)
+        latent = jnp.maximum(summed[s, :], slope[...] * summed[s, :]).astype(BF16)
+        narrowed[s, :] = jnp.where(masked[s, :] > 0, replaced, mm(latent, weight[...])).astype(BF16)
     half, narrow = folded.shape[1], narrowed.shape[1]
     both = jnp.concatenate([narrowed[:half, :], narrowed[half:, :]], axis=1)
     pair = mm(folded[...], both)
@@ -254,9 +260,11 @@
 def final_kernel(routes, blk, total, halo, targets, scale, wanted, *rest):
     rebuilt, error, pool = rest[-3:]
     fill_pool(routes, rest, pool)
-    summed = total[...] + mm(halo[...], pool[...])
+    half = total.shape[0] // 2
+    sums = [total[r : r + half, :] + mm(halo[r : r + half, :], pool[...]) for r in (0, half)]
     for b in range(scale.shape[0]):
-        rounded = summed[b * blk : (b + 1) * blk, :].astype(BF16)
+        top = b * blk // half
+        rounded = sums[top][b * blk - top * half : (b + 1) * blk - top * half, :].astype(BF16)
         rebuilt[b * blk : (b + 1) * blk, :] = rounded
         u = rounded.astype(F32)
         x = targets[b * blk : (b + 1) * blk, :].astype(F32)
@@ -339,23 +347,10 @@
     blocks = rows // blk
     m_dom, m_grp = send_rows.shape[1], cross_rows.shape[1]
     halo_rows = n_dom * m_dom + n_grp * m_grp
-    chunks = 4
-    to_stage = (
-        local_tiles,
-        local_src,
-        local_dst,
-        halo_tiles,
-        halo_src,
-        halo_dst,
-        enc_bias[None, :],
-        enc_slope[None, :],
-        dec_token,
-        dec_weight,
-        dec_bias[None, :],
-        targets,
-        mask_nodes,
-        remask_nodes,
-    )
+    chunks = 2
+    early = (local_tiles, local_src, local_dst, enc_bias[None, :], remask_nodes)
+    late = (halo_tiles, halo_src, halo_dst, enc_slope[None, :], dec_token, dec_weight)
+    late += (dec_bias[None, :], targets, mask_nodes)
 
     def like(arrays):
         return [sds(x.shape, x.dtype) for x in arrays]
@@ -363,27 +358,29 @@
     def scalars(*arrays):
         return [pltpu.SMEM(x.shape, i32) for x in arrays] + [pltpu.SemaphoreType.DMA((len(arrays),))]
 
-    fed = [pltpu.with_memory_space_constraint(x, pltpu.HBM) for x in (hidden, enc_weight, send_rows, cross_rows, *to_stage)]
+    def in_hbm(arrays):
+        return [pltpu.with_memory_space_constraint(x, pltpu.HBM) for x in arrays]
+
+    fed = in_hbm((hidden, enc_weight, send_rows, cross_rows, *early))
     wide, thin = routes(n_dom, n_grp, m_dom, m_grp)
     slots = [sds((size, width), BF16) for route in wide for size in route.sizes()[1:]]
     encoded, send_rows, cross_rows, *outs = call(
-        functools.partial(encode_kernel, wide, len(to_stage), chunks),
-        [sds((rows, width), BF16)] + like((send_rows, cross_rows)) + slots + like(to_stage),
+        functools.partial(encode_kernel, wide, len(early), chunks),
+        [sds((rows, width), BF16)] + like((send_rows, cross_rows)) + slots + like(early),
         [HBM] * len(fed),
         fed,
         [
             pltpu.VMEM(hidden.shape, BF16),
             pltpu.VMEM(enc_weight.shape, BF16),
             pltpu.VMEM(((n_dom - 1) * m_dom + (n_grp - 1) * m_grp, rows), BF16),
-            pltpu.SemaphoreType.DMA((3 + chunks + len(to_stage),)),
+            pltpu.SemaphoreType.DMA((3 + chunks + len(early),)),
         ],
     )
     sends, staged = outs[: len(slots)], outs[len(slots) :]
-    tiles, src, dst, halo_edges, halo_from, halo_to = staged[:6]
-    enc_bias, enc_slope, dec_token, dec_weight, dec_bias, targets, mask_nodes, remask_nodes = staged[6:]
+    tiles, src, dst, enc_bias, remask_nodes = staged
     passing, came = send_out(wide, sends)
-    total, folded, upper, masked, *stay = call(
-        functools.partial(local_kernel, wide),
+    total, folded, upper, masked, *outs = call(
+        functools.partial(local_kernel, wide, len(late)),
         [
             sds((rows, width), F32),
             sds((halo_rows, rows // 2), BF16),
@@ -391,11 +388,19 @@
             sds((rows, narrow), F32),
             sds((m_dom, width), BF16),
             sds((m_grp, width), BF16),
+        ]
+        + like(late),
+        [VMEM] * 8 + [SMEM] + [HBM] * len(late),
+        (encoded, tiles, src, dst, enc_bias, remask_nodes, send_rows, cross_rows, local_count, *in_hbm(late)),
+        [
+            pltpu.VMEM((n_tiles, blk, width), F32),
+            pltpu.SMEM(src.shape, i32),
+            pltpu.SMEM(dst.shape, i32),
+            pltpu.SemaphoreType.DMA((2 + len(late),)),
         ],
-        [VMEM] * 8 + [SMEM],
-        (encoded, tiles, src, dst, enc_bias, remask_nodes, send_rows, cross_rows, local_count),
-        [pltpu.VMEM((n_tiles, blk, width), F32)] + scalars(src, dst),
-    )
+    )
+    stay, staged = outs[:2], outs[2:]
+    halo_edges, halo_from, halo_to, enc_slope, dec_token, dec_weight, dec_bias, targets, mask_nodes = staged
     came = send_on(wide, passing, came)
     args = (total, halo_edges, halo_from, halo_to, folded, upper, masked, enc_slope, dec_token, dec_weight)
     args += (stay[0], *came[0], stay[1], *came[1])

time: 45.1 us -> 43.2 us (0.958)
  waiting for transfers between devices: 9.69 us -> 7.34 us
  starting transfers between devices: 23.5 us -> 24.4 us
  Pallas kernels: 10.4 us -> 9.9 us
    ppermute x16, waiting for transfers between devices: 9.69 us -> 7.34 us  [permute(): lax.ppermute(x, self.name, [(j, self.partner(j, step)) for j in range(sel...]
    ppermute x16, starting transfers between devices: 23.5 us -> 24.4 us  [permute(): lax.ppermute(x, self.name, [(j, self.partner(j, step)) for j in range(sel...]
    pallas_call x7, Pallas kernels: 10.4 us -> 9.9 us  [call(): pl.pallas_call(kernel, out_shape=tuple(outs), in_specs=specs, out_specs=t...]
  transfers between devices with their start and end apart: 16 -> 16, of which waited for: 4 -> 4; matrix products, arithmetic and copies ran while one was open for 0% -> 0% of each run, Pallas kernels for 6% -> 8%
where the time goes in v2:
time: 43.2 us; the launch traced here: 43 us
  starting transfers between devices  24.4 us (56%)
  Pallas kernels  9.9 us (23%)
  waiting for transfers between devices  7.34 us (17%)
  between operations  1.38 us (3%)
    ppermute x16, starting transfers between devices, permute(): lax.ppermute(x, self.name, [(j, self.partner(j, step)) for j in range(sel...  24.4 us
    pallas_call x7, Pallas kernels, call(): pl.pallas_call(kernel, out_shape=tuple(outs), in_specs=specs, out_specs=t...  9.9 us
    ppermute x16, waiting for transfers between devices, permute(): lax.ppermute(x, self.name, [(j, self.partner(j, step)) for j in range(sel...  7.34 us
  transfers between devices with their start and end apart: 16, of which 4 were waited for; matrix products, arithmetic and copies ran while one was open for 0% of the time, Pallas kernels for 8%

profile of v2, /device:TPU:0, one launch (start us, length us, event | category | flops | bytes accessed | tf_op | source)
XLA Modules:
  0.0 43.0 jit_solution(6448757348256622628)
XLA Ops:
  0.6 3.1 %shard_map.194 = (bf16[1024,512]{1,0:T(8,128)(2,1)S(1)}, s32[8,64]{1,0:T(8,128)S(1)}, s32[4,128]{1,0:T(4,128)S(1)}, bf16[64,512]{1,0:T(8,128)(2,1)S(1)}, bf16[64...) custom-call(bf16[1024,512]{1,0:T(8,128)(2,1)} %refs_0_.2, ...), custom_call_target="tpu_custom_call" | custom-call | flops 1000000000 | bytes 1048576 | tf_op jit(solution)/shard_map/pallas_call | solution.py:278
  3.8 3.0 %collective-permute-start = (bf16[64,512]{1,0:T(8,128)(2,1)S(1)}, bf16[64,512]{1,0:T(8,128)(2,1)S(1)}, u32[]{:S(2)}, u32[]{:S(2)}) collective-permute-start(bf16[64,512]{1,0:T(8,128)(2,1)S(1)} %get-tuple-element.71), channel_id=1, source_target_pairs={{0,1},{1,0},{2,3},{3,2},{4,5},{5,4},{6,7},{7,6},{8,9},{9,8},{10,11... | collective-permute-start | bytes 196616 | tf_op jit(solution)/shard_map/ppermute | solution.py:36
  6.8 1.6 %collective-permute-start.1 = (bf16[64,512]{1,0:T(8,128)(2,1)S(1)}, bf16[64,512]{1,0:T(8,128)(2,1)S(1)}, u32[]{:S(2)}, u32[]{:S(2)}) collective-permute-start(bf16[64,512]{1,0:T(8,128)(2,1)S(1)} %get-tuple-element.72), channel_id=1, source_target_pairs={{0,2},{1,3},{2,0},{3,1},{4,6},{5,7},{6,4},{7,5},{8,10},{9,11},{10,... | collective-permute-start | bytes 196616 | tf_op jit(solution)/shard_map/ppermute | solution.py:36
  8.4 0.0 collective-permute-start.2
  8.4 3.0 %collective-permute-start.3 = (bf16[64,512]{1,0:T(8,128)(2,1)S(1)}, bf16[64,512]{1,0:T(8,128)(2,1)S(1)}, u32[]{:S(2)}, u32[]{:S(2)}) collective-permute-start(bf16[64,512]{1,0:T(8,128)(2,1)S(1)} %get-tuple-element.74), channel_id=1, source_target_pairs={{0,4},{1,5},{2,6},{3,7},{4,0},{5,1},{6,2},{7,3},{8,12},{9,13},{10,... | collective-permute-start | bytes 196616 | tf_op jit(solution)/shard_map/ppermute | solution.py:36
  11.4 1.3 %collective-permute-start.4 = (bf16[64,512]{1,0:T(8,128)(2,1)S(1)}, bf16[64,512]{1,0:T(8,128)(2,1)S(1)}, u32[]{:S(2)}, u32[]{:S(2)}) collective-permute-start(bf16[64,512]{1,0:T(8,128)(2,1)S(1)} %get-tuple-element.75), channel_id=1, source_target_pairs={{0,5},{1,4},{2,7},{3,6},{4,1},{5,0},{6,3},{7,2},{8,13},{9,12},{10,... | collective-permute-start | bytes 196616 | tf_op jit(solution)/shard_map/ppermute | solution.py:36
  12.7 0.0 collective-permute-done.rest_1_
  12.7 0.0 collective-permute-start.7
  12.7 0.0 collective-permute-done.1.rest_2_
  12.7 1.6 %collective-permute-start.8 = (bf16[128,512]{1,0:T(8,128)(2,1)S(1)}, bf16[128,512]{1,0:T(8,128)(2,1)S(1)}, u32[]{:S(2)}, u32[]{:S(2)}) collective-permute-start(bf16[128,512]{1,0:T(8,128)(2,1)S(1)} %get-tuple-element.80), channel_id=1, source_target_pairs={{0,16},{8,24},{16,0},{24,8},{1,17},{9,25},{17,1},{25,9},{2,18},{10... | collective-permute-start | bytes 393224 | tf_op jit(solution)/shard_map/ppermute | solution.py:36
  14.3 0.0 collective-permute-done.2.rest_3_
  14.3 0.3 collective-permute-start.9
  15.2 4.4 %collective-permute-start.5 = (bf16[64,512]{1,0:T(8,128)(2,1)S(1)}, bf16[64,512]{1,0:T(8,128)(2,1)S(1)}, u32[]{:S(2)}, u32[]{:S(2)}) collective-permute-start(bf16[64,512]{1,0:T(8,128)(2,1)S(1)} %get-tuple-element.76), channel_id=1, source_target_pairs={{0,6},{1,7},{2,4},{3,5},{4,2},{5,3},{6,0},{7,1},{8,14},{9,15},{10,... | collective-permute-start | bytes 196616 | tf_op jit(solution)/shard_map/ppermute | solution.py:36
  19.6 0.0 collective-permute-done.4.rest_5_
  19.6 1.8 %collective-permute-start.6 = (bf16[64,512]{1,0:T(8,128)(2,1)S(1)}, bf16[64,512]{1,0:T(8,128)(2,1)S(1)}, u32[]{:S(2)}, u32[]{:S(2)}) collective-permute-start(bf16[64,512]{1,0:T(8,128)(2,1)S(1)} %get-tuple-element.77), channel_id=1, source_target_pairs={{0,7},{1,6},{2,5},{3,4},{4,3},{5,2},{6,1},{7,0},{8,15},{9,14},{10,... | collective-permute-start | bytes 196616 | tf_op jit(solution)/shard_map/ppermute | solution.py:36
  21.3 2.0 %shard_map.195 = (f32[1024,512]{1,0:T(8,128)S(1)}, bf16[1024,512]{1,0:T(8,128)(2,1)S(1)}, f32[1024,128]{1,0:T(8,128)S(1)}, f32[1024,128]{1,0:T(8,128)S(1)}, bf16...) custom-call(bf16[1024,512]{1,0:T(8,128)(2,1)S(1)} %get-tuple-element, ...), custom_call_target="tpu_custom_call" | custom-call | flops 1000000000 | bytes 1048576 | tf_op jit(solution)/shard_map/pallas_call | solution.py:278
  23.3 3.2 %collective-permute-done.6.rest_7_ = bf16[64,512]{1,0:T(8,128)(2,1)S(1)} collective-permute-done((bf16[64,512]{1,0:T(8,128)(2,1)S(1)}, bf16[64,512]{1,0:T(8,128)(2,1)S(1)}, u32[]{:S(2)}, u32[]{:S(2)}) %collective-permute-start.6) | collective-permute-done | bytes 65568 | tf_op jit(solution)/shard_map/ppermute | solution.py:36
  26.5 0.0 collective-permute-done.7.rest_9_
  26.5 0.0 collective-permute-done.8.rest_10_
  26.5 0.0 collective-permute-done.9.rest_11_
  26.5 2.0 %shard_map.196 = (f32[1024,512]{1,0:T(8,128)S(1)}, bf16[1024,128]{1,0:T(8,128)(2,1)S(1)}, bf16[64,128]{1,0:T(8,128)(2,1)S(1)}, bf16[64,128]{1,0:T(8,128)(2,1)S(1...) custom-call(f32[1024,512]{1,0:T(8,128)S(1)} %get-tuple-element.60.to, ...), custom_call_target="tpu_custom_call", output_to_operand_aliasing={{0}: (0, {})} | custom-call | flops 1000000000 | bytes 1048576 | tf_op jit(solution)/shard_map/pallas_call | solution.py:278
  28.5 0.1 collective-permute-start.10
  28.6 2.4 %collective-permute-start.11 = (bf16[128,128]{1,0:T(8,128)(2,1)S(1)}, bf16[128,128]{1,0:T(8,128)(2,1)S(1)}, u32[]{:S(2)}, u32[]{:S(2)}) collective-permute-start(bf16[128,128]{1,0:T(8,128)(2,1)S(1)} %get-tuple-element.92), channel_id=1, source_target_pairs={{0,4},{1,5},{2,6},{3,7},{4,0},{5,1},{6,2},{7,3},{8,12},{9,13},{10,... | collective-permute-start | bytes 98312 | tf_op jit(solution)/shard_map/ppermute | solution.py:36
  31.0 2.0 %collective-permute-start.12 = (bf16[128,128]{1,0:T(8,128)(2,1)S(1)}, bf16[128,128]{1,0:T(8,128)(2,1)S(1)}, u32[]{:S(2)}, u32[]{:S(2)}) collective-permute-start(bf16[128,128]{1,0:T(8,128)(2,1)S(1)} %get-tuple-element.93), channel_id=1, source_target_pairs={{0,6},{1,7},{2,4},{3,5},{4,2},{5,3},{6,0},{7,1},{8,14},{9,15},{10,... | collective-permute-start | bytes 98312 | tf_op jit(solution)/shard_map/ppermute | solution.py:36
  33.0 1.5 %collective-permute-start.13 = (bf16[256,128]{1,0:T(8,128)(2,1)S(1)}, bf16[256,128]{1,0:T(8,128)(2,1)S(1)}, u32[]{:S(2)}, u32[]{:S(2)}) collective-permute-start(bf16[256,128]{1,0:T(8,128)(2,1)S(1)} %get-tuple-element.96), channel_id=1, source_target_pairs={{0,16},{8,24},{16,0},{24,8},{1,17},{9,25},{17,1},{25,9},{2,18},{10... | collective-permute-start | bytes 196616 | tf_op jit(solution)/shard_map/ppermute | solution.py:36
  34.5 0.4 shard_map.198
  34.9 1.7 %collective-permute-done.12.refs_3_.rest_3_ = bf16[128,128]{1,0:T(8,128)(2,1)S(1)} collective-permute-done((bf16[128,128]{1,0:T(8,128)(2,1)S(1)}, bf16[128,128]{1,0:T(8,128)(2,1)S(1)}, u32[]{:S(2)}, u32[]{:S(2)}) %collective-permute-start.12) | collective-permute-done | bytes 32800 | tf_op jit(solution)/shard_map/ppermute | solution.py:36
  36.7 0.6 %collective-permute-done.13.refs_5_.rest_6_ = bf16[256,128]{1,0:T(8,128)(2,1)S(1)} collective-permute-done((bf16[256,128]{1,0:T(8,128)(2,1)S(1)}, bf16[256,128]{1,0:T(8,128)(2,1)S(1)}, u32[]{:S(2)}, u32[]{:S(2)}) %collective-permute-start.13) | collective-permute-done | bytes 65568 | tf_op jit(solution)/shard_map/ppermute | solution.py:36
  37.2 1.6 %collective-permute-start.14 = (bf16[256,128]{1,0:T(8,128)(2,1)S(1)}, bf16[256,128]{1,0:T(8,128)(2,1)S(1)}, u32[]{:S(2)}, u32[]{:S(2)}) collective-permute-start(bf16[256,128]{1,0:T(8,128)(2,1)S(1)} %get-tuple-element.97), channel_id=1, source_target_pairs={{0,1},{1,0},{2,3},{3,2},{4,5},{5,4},{6,7},{7,6},{8,9},{9,8},{10,11... | collective-permute-start | bytes 196616 | tf_op jit(solution)/shard_map/ppermute | solution.py:36
  38.8 0.9 %shard_map.197 = (f32[1024,128]{1,0:T(8,128)S(1)}, bf16[1024,1024]{1,0:T(8,128)(2,1)S(1)}) custom-call(bf16[1024,128]{1,0:T(8,128)(2,1)S(1)} %get-tuple-element.82.narrowed, bf16[12,128,128]{2,1,0:T(8,128)(2,1)S(1)} %get-tuple-element.53.tiles, s32[1,12]{1,0:T(1,128)S(1)} %get-tuple-element.54.src_v, s32[1,12]{1,0:T(1,128)S(1)} %get-tuple-element.55.dst_v, ...), custom_call_target="tpu_custom_call" | custom-call | flops 1000000000 | bytes 1048576 | tf_op jit(solution)/shard_map/pallas_call | solution.py:278
  39.8 1.8 %collective-permute-done.14.rest_4_ = bf16[256,128]{1,0:T(8,128)(2,1)S(1)} collective-permute-done((bf16[256,128]{1,0:T(8,128)(2,1)S(1)}, bf16[256,128]{1,0:T(8,128)(2,1)S(1)}, u32[]{:S(2)}, u32[]{:S(2)}) %collective-permute-start.14) | collective-permute-done | bytes 65568 | tf_op jit(solution)/shard_map/ppermute | solution.py:36
  41.6 1.5 %shard_map.200 = (bf16[1024,128]{1,0:T(8,128)(2,1)}, f32[8,128]{1,0:T(8,128)}) custom-call(f32[1024,128]{1,0:T(8,128)S(1)} %get-tuple-element.84.total, bf16[1024,1024]{1,0:T(8,128)(2,1)S(1)} %get-tuple-element.85.halo, bf16[1024,128]{1,0:T(8,128)(2,1)S(1)} %get-tuple-element.86.targets, f32[8,128]{1,0:T(8,128)S(1)} %get-tuple-element.88.scale, ...), custom_call_target="tpu_custom_call" | custom-call | flops 1000000000 | bytes 1048576 | tf_op jit(solution)/shard_map/pallas_call | solution.py:278
  (7 shorter events, 0.0 us)
Async XLA Ops:
  3.8 8.9 %collective-permute-start = (bf16[64,512]{1,0:T(8,128)(2,1)S(1)}, bf16[64,512]{1,0:T(8,128)(2,1)S(1)}, u32[]{:S(2)}, u32[]{:S(2)}) collective-permute-start(bf16[64,512]{1,0:T(8,128)(2,1)S(1)} %get-tuple-element.71), channel_id=1, source_target_pairs={{0,1},{1,0},{2,3},{3,2},{4,5},{5,4},{6,7},{7,6},{8,9},{9,8},{10,11... | collective-permute-start | bytes 196616 | tf_op jit(solution)/shard_map/ppermute | solution.py:36
  6.8 5.9 %collective-permute-start.1 = (bf16[64,512]{1,0:T(8,128)(2,1)S(1)}, bf16[64,512]{1,0:T(8,128)(2,1)S(1)}, u32[]{:S(2)}, u32[]{:S(2)}) collective-permute-start(bf16[64,512]{1,0:T(8,128)(2,1)S(1)} %get-tuple-element.72), channel_id=1, source_target_pairs={{0,2},{1,3},{2,0},{3,1},{4,6},{5,7},{6,4},{7,5},{8,10},{9,11},{10,... | collective-permute-start | bytes 196616 | tf_op jit(solution)/shard_map/ppermute | solution.py:36
  8.4 5.9 %collective-permute-start.2 = (bf16[64,512]{1,0:T(8,128)(2,1)S(1)}, bf16[64,512]{1,0:T(8,128)(2,1)S(1)}, u32[]{:S(2)}, u32[]{:S(2)}) collective-permute-start(bf16[64,512]{1,0:T(8,128)(2,1)S(1)} %get-tuple-element.73), channel_id=1, source_target_pairs={{0,3},{1,2},{2,1},{3,0},{4,7},{5,6},{6,5},{7,4},{8,11},{9,10},{10,... | collective-permute-start | bytes 196616 | tf_op jit(solution)/shard_map/ppermute | solution.py:36
  8.4 6.8 %collective-permute-start.3 = (bf16[64,512]{1,0:T(8,128)(2,1)S(1)}, bf16[64,512]{1,0:T(8,128)(2,1)S(1)}, u32[]{:S(2)}, u32[]{:S(2)}) collective-permute-start(bf16[64,512]{1,0:T(8,128)(2,1)S(1)} %get-tuple-element.74), channel_id=1, source_target_pairs={{0,4},{1,5},{2,6},{3,7},{4,0},{5,1},{6,2},{7,3},{8,12},{9,13},{10,... | collective-permute-start | bytes 196616 | tf_op jit(solution)/shard_map/ppermute | solution.py:36
  11.4 8.2 %collective-permute-start.4 = (bf16[64,512]{1,0:T(8,128)(2,1)S(1)}, bf16[64,512]{1,0:T(8,128)(2,1)S(1)}, u32[]{:S(2)}, u32[]{:S(2)}) collective-permute-start(bf16[64,512]{1,0:T(8,128)(2,1)S(1)} %get-tuple-element.75), channel_id=1, source_target_pairs={{0,5},{1,4},{2,7},{3,6},{4,1},{5,0},{6,3},{7,2},{8,13},{9,12},{10,... | collective-permute-start | bytes 196616 | tf_op jit(solution)/shard_map/ppermute | solution.py:36
  12.7 13.9 %collective-permute-start.7 = (bf16[128,512]{1,0:T(8,128)(2,1)S(1)}, bf16[128,512]{1,0:T(8,128)(2,1)S(1)}, u32[]{:S(2)}, u32[]{:S(2)}) collective-permute-start(bf16[128,512]{1,0:T(8,128)(2,1)S(1)} %get-tuple-element.79), channel_id=1, source_target_pairs={{0,8},{8,0},{16,24},{24,16},{1,9},{9,1},{17,25},{25,17},{2,10},{10... | collective-permute-start | bytes 393224 | tf_op jit(solution)/shard_map/ppermute | solution.py:36
  12.7 13.9 %collective-permute-start.8 = (bf16[128,512]{1,0:T(8,128)(2,1)S(1)}, bf16[128,512]{1,0:T(8,128)(2,1)S(1)}, u32[]{:S(2)}, u32[]{:S(2)}) collective-permute-start(bf16[128,512]{1,0:T(8,128)(2,1)S(1)} %get-tuple-element.80), channel_id=1, source_target_pairs={{0,16},{8,24},{16,0},{24,8},{1,17},{9,25},{17,1},{25,9},{2,18},{10... | collective-permute-start | bytes 393224 | tf_op jit(solution)/shard_map/ppermute | solution.py:36
  14.3 12.3 %collective-permute-start.9 = (bf16[128,512]{1,0:T(8,128)(2,1)S(1)}, bf16[128,512]{1,0:T(8,128)(2,1)S(1)}, u32[]{:S(2)}, u32[]{:S(2)}) collective-permute-start(bf16[128,512]{1,0:T(8,128)(2,1)S(1)} %get-tuple-element.81), channel_id=1, source_target_pairs={{0,24},{8,16},{16,8},{24,0},{1,25},{9,17},{17,9},{25,1},{2,26},{10... | collective-permute-start | bytes 393224 | tf_op jit(solution)/shard_map/ppermute | solution.py:36
  15.2 8.1 %collective-permute-start.5 = (bf16[64,512]{1,0:T(8,128)(2,1)S(1)}, bf16[64,512]{1,0:T(8,128)(2,1)S(1)}, u32[]{:S(2)}, u32[]{:S(2)}) collective-permute-start(bf16[64,512]{1,0:T(8,128)(2,1)S(1)} %get-tuple-element.76), channel_id=1, source_target_pairs={{0,6},{1,7},{2,4},{3,5},{4,2},{5,3},{6,0},{7,1},{8,14},{9,15},{10,... | collective-permute-start | bytes 196616 | tf_op jit(solution)/shard_map/ppermute | solution.py:36
  19.6 7.0 %collective-permute-start.6 = (bf16[64,512]{1,0:T(8,128)(2,1)S(1)}, bf16[64,512]{1,0:T(8,128)(2,1)S(1)}, u32[]{:S(2)}, u32[]{:S(2)}) collective-permute-start(bf16[64,512]{1,0:T(8,128)(2,1)S(1)} %get-tuple-element.77), channel_id=1, source_target_pairs={{0,7},{1,6},{2,5},{3,4},{4,3},{5,2},{6,1},{7,0},{8,15},{9,14},{10,... | collective-permute-start | bytes 196616 | tf_op jit(solution)/shard_map/ppermute | solution.py:36
  28.5 6.4 %collective-permute-start.10 = (bf16[128,128]{1,0:T(8,128)(2,1)S(1)}, bf16[128,128]{1,0:T(8,128)(2,1)S(1)}, u32[]{:S(2)}, u32[]{:S(2)}) collective-permute-start(bf16[128,128]{1,0:T(8,128)(2,1)S(1)} %get-tuple-element.91), channel_id=1, source_target_pairs={{0,2},{1,3},{2,0},{3,1},{4,6},{5,7},{6,4},{7,5},{8,10},{9,11},{10,... | collective-permute-start | bytes 98312 | tf_op jit(solution)/shard_map/ppermute | solution.py:36
  28.6 6.3 %collective-permute-start.11 = (bf16[128,128]{1,0:T(8,128)(2,1)S(1)}, bf16[128,128]{1,0:T(8,128)(2,1)S(1)}, u32[]{:S(2)}, u32[]{:S(2)}) collective-permute-start(bf16[128,128]{1,0:T(8,128)(2,1)S(1)} %get-tuple-element.92), channel_id=1, source_target_pairs={{0,4},{1,5},{2,6},{3,7},{4,0},{5,1},{6,2},{7,3},{8,12},{9,13},{10,... | collective-permute-start | bytes 98312 | tf_op jit(solution)/shard_map/ppermute | solution.py:36
  31.0 5.7 %collective-permute-start.12 = (bf16[128,128]{1,0:T(8,128)(2,1)S(1)}, bf16[128,128]{1,0:T(8,128)(2,1)S(1)}, u32[]{:S(2)}, u32[]{:S(2)}) collective-permute-start(bf16[128,128]{1,0:T(8,128)(2,1)S(1)} %get-tuple-element.93), channel_id=1, source_target_pairs={{0,6},{1,7},{2,4},{3,5},{4,2},{5,3},{6,0},{7,1},{8,14},{9,15},{10,... | collective-permute-start | bytes 98312 | tf_op jit(solution)/shard_map/ppermute | solution.py:36
  33.0 4.3 %collective-permute-start.13 = (bf16[256,128]{1,0:T(8,128)(2,1)S(1)}, bf16[256,128]{1,0:T(8,128)(2,1)S(1)}, u32[]{:S(2)}, u32[]{:S(2)}) collective-permute-start(bf16[256,128]{1,0:T(8,128)(2,1)S(1)} %get-tuple-element.96), channel_id=1, source_target_pairs={{0,16},{8,24},{16,0},{24,8},{1,17},{9,25},{17,1},{25,9},{2,18},{10... | collective-permute-start | bytes 196616 | tf_op jit(solution)/shard_map/ppermute | solution.py:36
  37.2 4.3 %collective-permute-start.14 = (bf16[256,128]{1,0:T(8,128)(2,1)S(1)}, bf16[256,128]{1,0:T(8,128)(2,1)S(1)}, u32[]{:S(2)}, u32[]{:S(2)}) collective-permute-start(bf16[256,128]{1,0:T(8,128)(2,1)S(1)} %get-tuple-element.97), channel_id=1, source_target_pairs={{0,1},{1,0},{2,3},{3,2},{4,5},{5,4},{6,7},{7,6},{8,9},{9,8},{10,11... | collective-permute-start | bytes 196616 | tf_op jit(solution)/shard_map/ppermute | solution.py:36
  38.8 2.8 %collective-permute-start.15 = (bf16[256,128]{1,0:T(8,128)(2,1)S(1)}, bf16[256,128]{1,0:T(8,128)(2,1)S(1)}, u32[]{:S(2)}, u32[]{:S(2)}) collective-permute-start(bf16[256,128]{1,0:T(8,128)(2,1)S(1)} %get-tuple-element.99), channel_id=1, source_target_pairs={{0,8},{8,0},{16,24},{24,16},{1,9},{9,1},{17,25},{25,17},{2,10},{10... | collective-permute-start | bytes 196616 | tf_op jit(solution)/shard_map/ppermute | solution.py:36
